TPU v7x, 32 devices: a whole 2x2x4 slice. The times are simulated.
32 devices in a mesh: sec: 4 (over y, x), strip: 8 (over z, core).
Axes of the slice: x: 2, y: 2, z: 4, core: 2. Of those that a mesh axis runs over, the one named last changes fastest.
Arguments:
- activations: bfloat16 [2, 4, 1, 2, 1, 256, 64, 512], P(None, 'sec', None, None, None, 'strip'), may hold values from 0 to 2
- relu_masks: int32 [2, 4, 1, 2, 1, 256, 64, 512], P(None, 'sec', None, None, None, 'strip'), may hold values 0 or 1
- grad_in: bfloat16 [2, 2, 1, 256, 64, 512], P(None, None, None, 'strip'), may hold values from -6 to 6
- mix_weight: bfloat16 [4, 1, 512, 512], P('sec'), may hold values from -0.375 to 0.375
- depth_kernel: bfloat16 [4, 1, 25, 512], P('sec'), may hold values from -1.25 to 1.25
Outputs:
- segment_grads: bfloat16 [2, 4, 2, 1, 256, 64, 512], P(None, 'sec', None, None, 'strip')
- mix_grad: float32 [4, 1, 512, 512], P('sec', None, 'strip')
- kernel_grad: float32 [4, 1, 25, 512], P('sec')
All inputs are finite; a program needn't handle non-finite values. No bound on the sum of `relu_masks` on one device may be relied on, other than what follows from the above.
Results may differ from a plain program's by a relative error of at most 0.025.
Values may be sent and summed in bfloat16 or wider, within the bound.
A program may use at most 192 MiB of HBM per device.

v0:
```python
import jax
import jax.numpy as jnp
from jax import lax
from jax.sharding import PartitionSpec as P

H = 256


def swapped(shard, axis, stride):
    return lax.ppermute(shard, axis, [(i, i ^ 1 << stride) for i in range(lax.axis_size(axis))])


def with_halo(cells, sides, width):
    for axis, dim in sides:
        count = lax.axis_size(axis)
        ends = count - 1
        head = lax.slice_in_dim(cells, 0, width, axis=dim)
        tail = lax.slice_in_dim(cells, cells.shape[dim] - width, cells.shape[dim], axis=dim)
        cells = jnp.concatenate(
            [
                lax.ppermute(tail, axis, [(i, (i + 1) % count) for i in range(ends)]),
                cells,
                lax.ppermute(head, axis, [((i + 1) % count, i) for i in range(ends)]),
            ],
            axis=dim,
        )
    return cells


def passed_along(shard, axis, by):
    length = lax.axis_size(axis)
    pairs = [(i, i + by) for i in range(length) if 0 <= i + by < length]
    return lax.ppermute(shard, axis, pairs)


def pad_columns(field):
    widths = [(0, 0)] * (field.ndim - 2) + [(2, 2), (0, 0)]
    return jnp.pad(field, widths)


def spread_taps(framed, kernels, rows, cols, base, sign):
    total = jnp.zeros(framed.shape[:2] + (rows, cols, framed.shape[-1]), jnp.float32)
    for row_tap in range(5):
        for col_tap in range(5):
            top = base + sign * row_tap
            left = base + sign * col_tap
            window = framed[:, :, top : top + rows, left : left + cols, :]
            factor = kernels[:, row_tap * 5 + col_tap][:, None, None, None, :].astype(jnp.float32)
            total = total + window.astype(jnp.float32) * factor
    return total


def tap_sums(back_mix, framed, rows, cols):
    terms = []
    for row_tap in range(5):
        for col_tap in range(5):
            window = framed[:, :, row_tap : row_tap + rows, col_tap : col_tap + cols, :]
            terms.append(
                jnp.sum(back_mix.astype(jnp.float32) * window.astype(jnp.float32), axis=(1, 2, 3))
            )
    return jnp.stack(terms, axis=1)


def pick_micro(stacked, chosen):
    return jax.vmap(
        lambda single, which: lax.dynamic_index_in_dim(single, which, 1, keepdims=False)
    )(stacked, chosen)


def store_slot(buffer, value, which, okay):
    previous = lax.dynamic_index_in_dim(buffer, which, 0, keepdims=False)
    return lax.dynamic_update_index_in_dim(buffer, jnp.where(okay, value, previous), which, 0)


def body(activations, relu_masks, grad_in, mix_weight, depth_kernel):
    sections = lax.axis_size("sec")
    position = lax.axis_index("sec")
    layers = activations.shape[2]
    micro = activations.shape[3]
    rows = activations.shape[5]
    cols = activations.shape[6]
    channels = activations.shape[7]
    levels = sections.bit_length() - 1
    packed = jnp.concatenate([mix_weight, depth_kernel], axis=2)
    mirrored = packed[0]
    for which_bit in range(levels):
        mirrored = swapped(mirrored, "sec", which_bit)
    weights = jnp.stack([mix_weight[0], mirrored[:, :channels]])
    kernels = jnp.stack([depth_kernel[0], mirrored[:, channels:]])
    padded_acts = pad_columns(with_halo(activations[:, 0], (("strip", 4),), 2))
    masks = relu_masks[:, 0]

    def tick_step(tick, carry):
        recv_down, recv_up, grads_w, grads_k, outputs = carry
        wanted = jnp.stack([tick - (sections - 1 - position), tick - position])
        valid = (wanted >= 0) & (wanted < micro)
        chosen = jnp.clip(wanted, 0, micro - 1)
        entry = jax.vmap(
            lambda single, which: lax.dynamic_index_in_dim(single, which, 0, keepdims=False)
        )(grad_in, chosen)
        upstream = jnp.stack(
            [
                jnp.where(position == sections - 1, entry[0], recv_down),
                jnp.where(position == 0, entry[1], recv_up),
            ]
        )
        acts_now = pick_micro(padded_acts, chosen)
        masks_now = pick_micro(masks, chosen)
        keep = valid[:, None, None]
        for layer in reversed(range(layers)):
            framed = acts_now[:, layer]
            kernel = kernels[:, layer]
            depth = spread_taps(framed, kernel, rows, cols, 0, 1).astype(jnp.bfloat16)
            gated = jnp.where(masks_now[:, layer] == 1, upstream, jnp.zeros_like(upstream))
            back_mix = jnp.einsum(
                "rbhwo,rio->rbhwi", gated, weights[:, layer], preferred_element_type=jnp.float32
            ).astype(jnp.bfloat16)
            weight_term = jnp.einsum(
                "rbhwi,rbhwo->rio", depth, gated, preferred_element_type=jnp.float32
            )
            edged = pad_columns(with_halo(back_mix, (("strip", 2),), 2))
            kernel_term = tap_sums(back_mix, framed, rows, cols)
            upstream = spread_taps(edged, kernel, rows, cols, 4, -1).astype(jnp.bfloat16)
            grads_w = grads_w.at[:, layer].add(jnp.where(keep, weight_term, 0.0))
            grads_k = grads_k.at[:, layer].add(jnp.where(keep, kernel_term, 0.0))
        outputs = jax.vmap(store_slot)(outputs, upstream, chosen, valid)
        recv_down = passed_along(upstream[0], "sec", -1)
        recv_up = passed_along(upstream[1], "sec", 1)
        return (recv_down, recv_up, grads_w, grads_k, outputs)

    blank = jnp.zeros(grad_in.shape[2:], jnp.bfloat16)
    start = (
        blank,
        blank,
        jnp.zeros((2, layers, channels, channels), jnp.float32),
        jnp.zeros((2, layers, 25, channels), jnp.float32),
        jnp.zeros(grad_in.shape, jnp.bfloat16),
    )
    finished = lax.fori_loop(0, micro + sections - 1, tick_step, start)
    grads_w, grads_k, outputs = (finished[2], finished[3], finished[4])
    factor = 1.0 / H
    shares = lax.psum_scatter(
        grads_w.astype(jnp.bfloat16), "strip", scatter_dimension=2, tiled=True
    ).astype(jnp.float32)
    kernel_all = lax.psum(grads_k.astype(jnp.bfloat16), "strip").astype(jnp.float32)
    share_rows = shares.shape[2]
    partner = jnp.concatenate([shares[1], kernel_all[1]], axis=1)
    for which_bit in range(levels):
        partner = swapped(partner.astype(jnp.bfloat16), "sec", which_bit).astype(partner.dtype)
    share_w = shares[0] + partner[:, :share_rows]
    full_k = kernel_all[0] + partner[:, share_rows:]
    return (outputs[:, None], (share_w * factor)[None], (full_k * factor)[None])


def solution(mesh):
    placed = (
        P(None, "sec", None, None, None, "strip", None, None),
        P(None, "sec", None, None, None, "strip", None, None),
        P(None, None, None, "strip", None, None),
        P("sec", None, None, None),
        P("sec", None, None, None),
    )
    return jax.shard_map(
        body,
        mesh=mesh,
        in_specs=placed,
        out_specs=(
            P(None, "sec", None, None, "strip", None, None),
            P("sec", None, "strip", None),
            P("sec", None, None, None),
        ),
        check_vma=False,
    )
```

profile of v0, /device:TPU:0, one launch (start us, length us, event | category | flops | bytes accessed | tf_op | source)
XLA Modules:
  0.0 1700.8 jit_solution(11052558939191926080)
XLA Ops:
  45.9 1555.1 %while.47 = (s32[]{:T(128)}, bf16[1,32,64,512]{3,2,1,0:T(8,128)(2,1)}, bf16[1,32,64,512]{3,2,1,0:T(8,128)(2,1)S(1)}, f32[2,1,512,512]{3,2,0,1:T(8,128)}, f32[2,1...) while((s32[]{:T(128)}, ...), condition=%wide.region_27.28_spmd.clone, body=%wide.region_0.27_spmd.clone.sunk | while | flops 4831063040 | bytes 484415488 | solution.py:139
  89.9 22.3 %fusion.181 = (f32[2,512]{1,0:T(2,128)S(1)}, f32[2,512]{1,0:T(2,128)S(1)}, f32[2,512]{1,0:T(2,128)S(1)}, f32[2,512]{1,0:T(2,128)S(1)}, f32[2,512]{1,0:T(2,128)S(...) fusion(bf16[2,1,36,68,512]{4,3,2,0,1:T(8,128)(2,1)} %bitcast.472, ...), kind=kOutput, calls=%fused_computation.128.clone.1 | convolution fusion | flops 2202002432 | bytes 47214592 | tf_op jit(solution)/shard_map/while/body/eval_jaxpr/rbhwo,rio->rbhwi/dot_general | solution.py:115
  118.1 42.8 %fusion.187 = (f32[2,512]{1,0:T(2,128)S(1)}, f32[2,512]{1,0:T(2,128)S(1)}, f32[2,512]{1,0:T(2,128)S(1)}, f32[2,512]{1,0:T(2,128)S(1)}, f32[2,512]{1,0:T(2,128)S(...) fusion(bf16[2,32,64,512]{3,2,1,0:T(8,128)(2,1)} %get-tuple-elem, ...), kind=kLoop, calls=%fused_computation.129.clone.1 | loop fusion | flops 115324928 | bytes 79765504 | tf_op jit(solution)/shard_map/while/body/eval_jaxpr/reduce_sum | solution.py:59
  173.4 49.7 %fusion.186 = bf16[2,32,64,512]{3,2,1,0:T(8,128)(2,1)} fusion(f32[2,512]{1,0:T(2,128)S(1)} %get-tuple-element.1020, f32[2,512]{1,0:T(2,128)S(1)} %get-tuple-element.1029, f32[2,512]{1,0:T(2,128)S(1)} %get-tuple-element.1030, f32[2,512]{1,0:T(2,128)S(1)} %get-tuple-element.1031, f32[2,512]{1,0:T(2,128)S(1)} %get-tuple-element.1032, ...), kind=kLoop, calls=%fused_computation.151.clone.clone.clone.2.clone.1 | loop fusion | flops 157286400 | bytes 109154304 | tf_op jit(solution)/shard_map/while/body/eval_jaxpr/rbhwi,rbhwo->rio/dot_general | solution.py:118
  229.6 38.2 %fusion.185 = (bf16[2,1,1,32,64,512]{5,4,3,2,1,0:T(8,128)(2,1)}, bf16[2,1,32,64,512]{4,3,2,0,1:T(8,128)(2,1)}) fusion(bf16[2,1,1,32,64,512]{5,4,3,2,1,0:T(8,128)(2,1)} %get-tuple-element.1019, pred[2]{0:T(512)(128)(4,1)S(1)} %compare_and_fusion.2, f32[2,512]{1,0:T(2,128)S(1)} %get-tuple-element.1020, bf16[2,1,36,68,512]{4,3,2,0,1:T(8,128)(2,1)S(1)} %fusion.183, ...), kind=kLoop, calls=%fused_computation.149.clone.1 | loop fusion | flops 167772160 | bytes 105484288 | tf_op jit(solution)/shard_map/while
  286.5 22.5 %while.52 = (s32[]{:T(128)}, bf16[2,2,1,32,64,512]{5,4,3,2,1,0:T(8,128)(2,1)}, s32[2,6]{1,0:T(2,128)S(1)}, bf16[2,1,1,32,64,512]{5,4,3,2,1,0:T(8,128)(2,1)}, s32[]{:T(128)}, /*index=5*/s32[6]{0:T(128)S(1)}) while((s32[]{:T(128)}, bf16[2,2,1,32,64,512]{5,4,3,2,1,0:T(8,128)(2,1)}, s32[2,6]{1,0:T(2,128)S(1)}, ...), condition=%wide.while_cond.6, body=%wide.while_body.6.sunk | while | flops 1048601 | bytes 6293270 | solution.py:72
  368.4 22.3 %fusion.181 = (f32[2,512]{1,0:T(2,128)S(1)}, f32[2,512]{1,0:T(2,128)S(1)}, f32[2,512]{1,0:T(2,128)S(1)}, f32[2,512]{1,0:T(2,128)S(1)}, f32[2,512]{1,0:T(2,128)S(...) fusion(bf16[2,1,36,68,512]{4,3,2,0,1:T(8,128)(2,1)} %bitcast.472, ...), kind=kOutput, calls=%fused_computation.128.clone.1 | convolution fusion | flops 2202002432 | bytes 47214592 | tf_op jit(solution)/shard_map/while/body/eval_jaxpr/rbhwo,rio->rbhwi/dot_general | solution.py:115
  396.2 42.8 %fusion.187 = (f32[2,512]{1,0:T(2,128)S(1)}, f32[2,512]{1,0:T(2,128)S(1)}, f32[2,512]{1,0:T(2,128)S(1)}, f32[2,512]{1,0:T(2,128)S(1)}, f32[2,512]{1,0:T(2,128)S(...) fusion(bf16[2,32,64,512]{3,2,1,0:T(8,128)(2,1)} %get-tuple-elem, ...), kind=kLoop, calls=%fused_computation.129.clone.1 | loop fusion | flops 115324928 | bytes 79765504 | tf_op jit(solution)/shard_map/while/body/eval_jaxpr/reduce_sum | solution.py:59
  451.6 49.7 %fusion.186 = bf16[2,32,64,512]{3,2,1,0:T(8,128)(2,1)} fusion(f32[2,512]{1,0:T(2,128)S(1)} %get-tuple-element.1020, f32[2,512]{1,0:T(2,128)S(1)} %get-tuple-element.1029, f32[2,512]{1,0:T(2,128)S(1)} %get-tuple-element.1030, f32[2,512]{1,0:T(2,128)S(1)} %get-tuple-element.1031, f32[2,512]{1,0:T(2,128)S(1)} %get-tuple-element.1032, ...), kind=kLoop, calls=%fused_computation.151.clone.clone.clone.2.clone.1 | loop fusion | flops 157286400 | bytes 109154304 | tf_op jit(solution)/shard_map/while/body/eval_jaxpr/rbhwi,rbhwo->rio/dot_general | solution.py:118
  507.7 38.2 %fusion.185 = (bf16[2,1,1,32,64,512]{5,4,3,2,1,0:T(8,128)(2,1)}, bf16[2,1,32,64,512]{4,3,2,0,1:T(8,128)(2,1)}) fusion(bf16[2,1,1,32,64,512]{5,4,3,2,1,0:T(8,128)(2,1)} %get-tuple-element.1019, pred[2]{0:T(512)(128)(4,1)S(1)} %compare_and_fusion.2, f32[2,512]{1,0:T(2,128)S(1)} %get-tuple-element.1020, bf16[2,1,36,68,512]{4,3,2,0,1:T(8,128)(2,1)S(1)} %fusion.183, ...), kind=kLoop, calls=%fused_computation.149.clone.1 | loop fusion | flops 167772160 | bytes 105484288 | tf_op jit(solution)/shard_map/while
  552.3 45.7 %collective-permute-start.3 = (bf16[1,32,64,512]{3,2,1,0:T(8,128)(2,1)}, bf16[1,32,64,512]{3,2,1,0:T(8,128)(2,1)S(1)}, u32[]{:S(2)}, u32[]{:S(2)}) collective-permute-start(bf16[1,32,64,512]{3,2,1,0:T(8,128)(2,1)} %get-tuple-element.1055), channel_id=1, source_target_pairs={{0,8},{8,16},{16,24},{1,9},{9,17},{17,25},{2,10},{10,18},{18,26},{... | collective-permute-start | bytes 6291464 | tf_op jit(solution)/shard_map/while/body/eval_jaxpr/ppermute | solution.py:33
  606.2 22.5 %while.52 = (s32[]{:T(128)}, bf16[2,2,1,32,64,512]{5,4,3,2,1,0:T(8,128)(2,1)}, s32[2,6]{1,0:T(2,128)S(1)}, bf16[2,1,1,32,64,512]{5,4,3,2,1,0:T(8,128)(2,1)}, s32[]{:T(128)}, /*index=5*/s32[6]{0:T(128)S(1)}) while((s32[]{:T(128)}, bf16[2,2,1,32,64,512]{5,4,3,2,1,0:T(8,128)(2,1)}, s32[2,6]{1,0:T(2,128)S(1)}, ...), condition=%wide.while_cond.6, body=%wide.while_body.6.sunk | while | flops 1048601 | bytes 6293270 | solution.py:72
  687.2 22.3 %fusion.181 = (f32[2,512]{1,0:T(2,128)S(1)}, f32[2,512]{1,0:T(2,128)S(1)}, f32[2,512]{1,0:T(2,128)S(1)}, f32[2,512]{1,0:T(2,128)S(1)}, f32[2,512]{1,0:T(2,128)S(...) fusion(bf16[2,1,36,68,512]{4,3,2,0,1:T(8,128)(2,1)} %bitcast.472, ...), kind=kOutput, calls=%fused_computation.128.clone.1 | convolution fusion | flops 2202002432 | bytes 47214592 | tf_op jit(solution)/shard_map/while/body/eval_jaxpr/rbhwo,rio->rbhwi/dot_general | solution.py:115
  715.3 42.8 %fusion.187 = (f32[2,512]{1,0:T(2,128)S(1)}, f32[2,512]{1,0:T(2,128)S(1)}, f32[2,512]{1,0:T(2,128)S(1)}, f32[2,512]{1,0:T(2,128)S(1)}, f32[2,512]{1,0:T(2,128)S(...) fusion(bf16[2,32,64,512]{3,2,1,0:T(8,128)(2,1)} %get-tuple-elem, ...), kind=kLoop, calls=%fused_computation.129.clone.1 | loop fusion | flops 115324928 | bytes 79765504 | tf_op jit(solution)/shard_map/while/body/eval_jaxpr/reduce_sum | solution.py:59
  770.7 49.7 %fusion.186 = bf16[2,32,64,512]{3,2,1,0:T(8,128)(2,1)} fusion(f32[2,512]{1,0:T(2,128)S(1)} %get-tuple-element.1020, f32[2,512]{1,0:T(2,128)S(1)} %get-tuple-element.1029, f32[2,512]{1,0:T(2,128)S(1)} %get-tuple-element.1030, f32[2,512]{1,0:T(2,128)S(1)} %get-tuple-element.1031, f32[2,512]{1,0:T(2,128)S(1)} %get-tuple-element.1032, ...), kind=kLoop, calls=%fused_computation.151.clone.clone.clone.2.clone.1 | loop fusion | flops 157286400 | bytes 109154304 | tf_op jit(solution)/shard_map/while/body/eval_jaxpr/rbhwi,rbhwo->rio/dot_general | solution.py:118
  826.8 38.2 %fusion.185 = (bf16[2,1,1,32,64,512]{5,4,3,2,1,0:T(8,128)(2,1)}, bf16[2,1,32,64,512]{4,3,2,0,1:T(8,128)(2,1)}) fusion(bf16[2,1,1,32,64,512]{5,4,3,2,1,0:T(8,128)(2,1)} %get-tuple-element.1019, pred[2]{0:T(512)(128)(4,1)S(1)} %compare_and_fusion.2, f32[2,512]{1,0:T(2,128)S(1)} %get-tuple-element.1020, bf16[2,1,36,68,512]{4,3,2,0,1:T(8,128)(2,1)S(1)} %fusion.183, ...), kind=kLoop, calls=%fused_computation.149.clone.1 | loop fusion | flops 167772160 | bytes 105484288 | tf_op jit(solution)/shard_map/while
  871.4 45.7 %collective-permute-start.3 = (bf16[1,32,64,512]{3,2,1,0:T(8,128)(2,1)}, bf16[1,32,64,512]{3,2,1,0:T(8,128)(2,1)S(1)}, u32[]{:S(2)}, u32[]{:S(2)}) collective-permute-start(bf16[1,32,64,512]{3,2,1,0:T(8,128)(2,1)} %get-tuple-element.1055), channel_id=1, source_target_pairs={{0,8},{8,16},{16,24},{1,9},{9,17},{17,25},{2,10},{10,18},{18,26},{... | collective-permute-start | bytes 6291464 | tf_op jit(solution)/shard_map/while/body/eval_jaxpr/ppermute | solution.py:33
  925.3 22.5 %while.52 = (s32[]{:T(128)}, bf16[2,2,1,32,64,512]{5,4,3,2,1,0:T(8,128)(2,1)}, s32[2,6]{1,0:T(2,128)S(1)}, bf16[2,1,1,32,64,512]{5,4,3,2,1,0:T(8,128)(2,1)}, s32[]{:T(128)}, /*index=5*/s32[6]{0:T(128)S(1)}) while((s32[]{:T(128)}, bf16[2,2,1,32,64,512]{5,4,3,2,1,0:T(8,128)(2,1)}, s32[2,6]{1,0:T(2,128)S(1)}, ...), condition=%wide.while_cond.6, body=%wide.while_body.6.sunk | while | flops 1048601 | bytes 6293270 | solution.py:72
  1006.3 22.3 %fusion.181 = (f32[2,512]{1,0:T(2,128)S(1)}, f32[2,512]{1,0:T(2,128)S(1)}, f32[2,512]{1,0:T(2,128)S(1)}, f32[2,512]{1,0:T(2,128)S(1)}, f32[2,512]{1,0:T(2,128)S(...) fusion(bf16[2,1,36,68,512]{4,3,2,0,1:T(8,128)(2,1)} %bitcast.472, ...), kind=kOutput, calls=%fused_computation.128.clone.1 | convolution fusion | flops 2202002432 | bytes 47214592 | tf_op jit(solution)/shard_map/while/body/eval_jaxpr/rbhwo,rio->rbhwi/dot_general | solution.py:115
  1034.4 42.8 %fusion.187 = (f32[2,512]{1,0:T(2,128)S(1)}, f32[2,512]{1,0:T(2,128)S(1)}, f32[2,512]{1,0:T(2,128)S(1)}, f32[2,512]{1,0:T(2,128)S(1)}, f32[2,512]{1,0:T(2,128)S(...) fusion(bf16[2,32,64,512]{3,2,1,0:T(8,128)(2,1)} %get-tuple-elem, ...), kind=kLoop, calls=%fused_computation.129.clone.1 | loop fusion | flops 115324928 | bytes 79765504 | tf_op jit(solution)/shard_map/while/body/eval_jaxpr/reduce_sum | solution.py:59
  1089.8 49.7 %fusion.186 = bf16[2,32,64,512]{3,2,1,0:T(8,128)(2,1)} fusion(f32[2,512]{1,0:T(2,128)S(1)} %get-tuple-element.1020, f32[2,512]{1,0:T(2,128)S(1)} %get-tuple-element.1029, f32[2,512]{1,0:T(2,128)S(1)} %get-tuple-element.1030, f32[2,512]{1,0:T(2,128)S(1)} %get-tuple-element.1031, f32[2,512]{1,0:T(2,128)S(1)} %get-tuple-element.1032, ...), kind=kLoop, calls=%fused_computation.151.clone.clone.clone.2.clone.1 | loop fusion | flops 157286400 | bytes 109154304 | tf_op jit(solution)/shard_map/while/body/eval_jaxpr/rbhwi,rbhwo->rio/dot_general | solution.py:118
  1145.9 38.2 %fusion.185 = (bf16[2,1,1,32,64,512]{5,4,3,2,1,0:T(8,128)(2,1)}, bf16[2,1,32,64,512]{4,3,2,0,1:T(8,128)(2,1)}) fusion(bf16[2,1,1,32,64,512]{5,4,3,2,1,0:T(8,128)(2,1)} %get-tuple-element.1019, pred[2]{0:T(512)(128)(4,1)S(1)} %compare_and_fusion.2, f32[2,512]{1,0:T(2,128)S(1)} %get-tuple-element.1020, bf16[2,1,36,68,512]{4,3,2,0,1:T(8,128)(2,1)S(1)} %fusion.183, ...), kind=kLoop, calls=%fused_computation.149.clone.1 | loop fusion | flops 167772160 | bytes 105484288 | tf_op jit(solution)/shard_map/while
  1190.5 45.7 %collective-permute-start.3 = (bf16[1,32,64,512]{3,2,1,0:T(8,128)(2,1)}, bf16[1,32,64,512]{3,2,1,0:T(8,128)(2,1)S(1)}, u32[]{:S(2)}, u32[]{:S(2)}) collective-permute-start(bf16[1,32,64,512]{3,2,1,0:T(8,128)(2,1)} %get-tuple-element.1055), channel_id=1, source_target_pairs={{0,8},{8,16},{16,24},{1,9},{9,17},{17,25},{2,10},{10,18},{18,26},{... | collective-permute-start | bytes 6291464 | tf_op jit(solution)/shard_map/while/body/eval_jaxpr/ppermute | solution.py:33
  1244.4 22.5 %while.52 = (s32[]{:T(128)}, bf16[2,2,1,32,64,512]{5,4,3,2,1,0:T(8,128)(2,1)}, s32[2,6]{1,0:T(2,128)S(1)}, bf16[2,1,1,32,64,512]{5,4,3,2,1,0:T(8,128)(2,1)}, s32[]{:T(128)}, /*index=5*/s32[6]{0:T(128)S(1)}) while((s32[]{:T(128)}, bf16[2,2,1,32,64,512]{5,4,3,2,1,0:T(8,128)(2,1)}, s32[2,6]{1,0:T(2,128)S(1)}, ...), condition=%wide.while_cond.6, body=%wide.while_body.6.sunk | while | flops 1048601 | bytes 6293270 | solution.py:72
  1325.4 22.3 %fusion.181 = (f32[2,512]{1,0:T(2,128)S(1)}, f32[2,512]{1,0:T(2,128)S(1)}, f32[2,512]{1,0:T(2,128)S(1)}, f32[2,512]{1,0:T(2,128)S(1)}, f32[2,512]{1,0:T(2,128)S(...) fusion(bf16[2,1,36,68,512]{4,3,2,0,1:T(8,128)(2,1)} %bitcast.472, ...), kind=kOutput, calls=%fused_computation.128.clone.1 | convolution fusion | flops 2202002432 | bytes 47214592 | tf_op jit(solution)/shard_map/while/body/eval_jaxpr/rbhwo,rio->rbhwi/dot_general | solution.py:115
  1353.5 42.8 %fusion.187 = (f32[2,512]{1,0:T(2,128)S(1)}, f32[2,512]{1,0:T(2,128)S(1)}, f32[2,512]{1,0:T(2,128)S(1)}, f32[2,512]{1,0:T(2,128)S(1)}, f32[2,512]{1,0:T(2,128)S(...) fusion(bf16[2,32,64,512]{3,2,1,0:T(8,128)(2,1)} %get-tuple-elem, ...), kind=kLoop, calls=%fused_computation.129.clone.1 | loop fusion | flops 115324928 | bytes 79765504 | tf_op jit(solution)/shard_map/while/body/eval_jaxpr/reduce_sum | solution.py:59
  1408.9 49.7 %fusion.186 = bf16[2,32,64,512]{3,2,1,0:T(8,128)(2,1)} fusion(f32[2,512]{1,0:T(2,128)S(1)} %get-tuple-element.1020, f32[2,512]{1,0:T(2,128)S(1)} %get-tuple-element.1029, f32[2,512]{1,0:T(2,128)S(1)} %get-tuple-element.1030, f32[2,512]{1,0:T(2,128)S(1)} %get-tuple-element.1031, f32[2,512]{1,0:T(2,128)S(1)} %get-tuple-element.1032, ...), kind=kLoop, calls=%fused_computation.151.clone.clone.clone.2.clone.1 | loop fusion | flops 157286400 | bytes 109154304 | tf_op jit(solution)/shard_map/while/body/eval_jaxpr/rbhwi,rbhwo->rio/dot_general | solution.py:118
  1465.0 38.2 %fusion.185 = (bf16[2,1,1,32,64,512]{5,4,3,2,1,0:T(8,128)(2,1)}, bf16[2,1,32,64,512]{4,3,2,0,1:T(8,128)(2,1)}) fusion(bf16[2,1,1,32,64,512]{5,4,3,2,1,0:T(8,128)(2,1)} %get-tuple-element.1019, pred[2]{0:T(512)(128)(4,1)S(1)} %compare_and_fusion.2, f32[2,512]{1,0:T(2,128)S(1)} %get-tuple-element.1020, bf16[2,1,36,68,512]{4,3,2,0,1:T(8,128)(2,1)S(1)} %fusion.183, ...), kind=kLoop, calls=%fused_computation.149.clone.1 | loop fusion | flops 167772160 | bytes 105484288 | tf_op jit(solution)/shard_map/while
  1509.7 45.7 %collective-permute-start.3 = (bf16[1,32,64,512]{3,2,1,0:T(8,128)(2,1)}, bf16[1,32,64,512]{3,2,1,0:T(8,128)(2,1)S(1)}, u32[]{:S(2)}, u32[]{:S(2)}) collective-permute-start(bf16[1,32,64,512]{3,2,1,0:T(8,128)(2,1)} %get-tuple-element.1055), channel_id=1, source_target_pairs={{0,8},{8,16},{16,24},{1,9},{9,17},{17,25},{2,10},{10,18},{18,26},{... | collective-permute-start | bytes 6291464 | tf_op jit(solution)/shard_map/while/body/eval_jaxpr/ppermute | solution.py:33
  1563.5 22.5 %while.52 = (s32[]{:T(128)}, bf16[2,2,1,32,64,512]{5,4,3,2,1,0:T(8,128)(2,1)}, s32[2,6]{1,0:T(2,128)S(1)}, bf16[2,1,1,32,64,512]{5,4,3,2,1,0:T(8,128)(2,1)}, s32[]{:T(128)}, /*index=5*/s32[6]{0:T(128)S(1)}) while((s32[]{:T(128)}, bf16[2,2,1,32,64,512]{5,4,3,2,1,0:T(8,128)(2,1)}, s32[2,6]{1,0:T(2,128)S(1)}, ...), condition=%wide.while_cond.6, body=%wide.while_body.6.sunk | while | flops 1048601 | bytes 6293270 | solution.py:72
  1605.1 27.1 %psum.7 = bf16[2,1,25,512]{3,2,1,0:T(8,128)(2,1)S(1)} all-reduce(bf16[2,1,25,512]{3,2,1,0:T(8,128)(2,1)S(1)} %convert_element_type.1180), channel_id=1, replica_groups=mesh['sec'=4,'strip'=8] {'strip'}, use_global_device_ids=true, to_apply=%region_29.30 | all-reduce | flops 25600 | bytes 102400 | tf_op jit(solution)/shard_map/psum | solution.py:145
  1632.2 49.6 %reduce-scatter.5.cloned.1.call-done = bf16[64,1024]{1,0:T(8,128)(2,1)} async-done(((bf16[512,1024]{1,0:T(8,128)(2,1)}), bf16[64,1024]{1,0:T(8,128)(2,1)}) %reduce-scatter.5.cloned.1.call-update) | async-done | bytes 131088
  (572 shorter events, 884.1 us)
Async XLA Ops:
  7.2 1674.7 %reduce-scatter.5.cloned.1.call-start = ((), (), s32[]{:S(2)}) async-start(), calls=%async_computation.1 | async-start | bytes 1179648
  8.3 15.7 collective-permute-start.4
  12.6 13.2 collective-permute-start.6
  14.1 11.7 collective-permute-start.7
  24.1 14.3 collective-permute-start.5
  113.3 110.6 %collective-permute-start = (bf16[2,1,2,64,512]{4,3,2,0,1:T(8,128)(2,1)S(1)}, bf16[2,1,2,64,512]{4,3,2,0,1:T(8,128)(2,1)S(1)}, u32[]{:S(2)}, u32[]{:S(2)}) collective-permute-start(bf16[2,1,2,64,512]{4,3,2,0,1:T(8,128)(2,1)S(1)} %get-tuple-element.1027), channel_id=1, source_target_pairs={{1,0},{2,1},{3,2},{4,3},{5,4},{6,5},{7,6},{9,8},{10,9},{11,10},{12... | collective-permute-start | bytes 786440 | tf_op jit(solution)/shard_map/while/body/eval_jaxpr/ppermute | solution.py:23
  114.6 109.3 %collective-permute-start.1 = (bf16[2,1,2,64,512]{4,3,2,0,1:T(8,128)(2,1)S(1)}, bf16[2,1,2,64,512]{4,3,2,0,1:T(8,128)(2,1)S(1)}, u32[]{:S(2)}, u32[]{:S(2)}) collective-permute-start(bf16[2,1,2,64,512]{4,3,2,0,1:T(8,128)(2,1)S(1)} %get-tuple-element.1028), channel_id=1, source_target_pairs={{0,1},{1,2},{2,3},{3,4},{4,5},{5,6},{6,7},{8,9},{9,10},{10,11},{11... | collective-permute-start | bytes 786440 | tf_op jit(solution)/shard_map/while/body/eval_jaxpr/ppermute | solution.py:21
  272.8 50.1 %collective-permute-start.2 = (bf16[1,32,64,512]{3,2,1,0:T(8,128)(2,1)}, bf16[1,32,64,512]{3,2,1,0:T(8,128)(2,1)}, u32[]{:S(2)}, u32[]{:S(2)}) collective-permute-start(bf16[1,32,64,512]{3,2,1,0:T(8,128)(2,1)} %get-tuple-element.1054), channel_id=1, source_target_pairs={{8,0},{16,8},{24,16},{9,1},{17,9},{25,17},{10,2},{18,10},{26,18},{... | collective-permute-start | bytes 6291464 | tf_op jit(solution)/shard_map/while/body/eval_jaxpr/ppermute | solution.py:33
  274.2 50.5 %collective-permute-start.3 = (bf16[1,32,64,512]{3,2,1,0:T(8,128)(2,1)}, bf16[1,32,64,512]{3,2,1,0:T(8,128)(2,1)S(1)}, u32[]{:S(2)}, u32[]{:S(2)}) collective-permute-start(bf16[1,32,64,512]{3,2,1,0:T(8,128)(2,1)} %get-tuple-element.1055), channel_id=1, source_target_pairs={{0,8},{8,16},{16,24},{1,9},{9,17},{17,25},{2,10},{10,18},{18,26},{... | collective-permute-start | bytes 6291464 | tf_op jit(solution)/shard_map/while/body/eval_jaxpr/ppermute | solution.py:33
  391.7 110.2 %collective-permute-start = (bf16[2,1,2,64,512]{4,3,2,0,1:T(8,128)(2,1)S(1)}, bf16[2,1,2,64,512]{4,3,2,0,1:T(8,128)(2,1)S(1)}, u32[]{:S(2)}, u32[]{:S(2)}) collective-permute-start(bf16[2,1,2,64,512]{4,3,2,0,1:T(8,128)(2,1)S(1)} %get-tuple-element.1027), channel_id=1, source_target_pairs={{1,0},{2,1},{3,2},{4,3},{5,4},{6,5},{7,6},{9,8},{10,9},{11,10},{12... | collective-permute-start | bytes 786440 | tf_op jit(solution)/shard_map/while/body/eval_jaxpr/ppermute | solution.py:23
  393.0 108.9 %collective-permute-start.1 = (bf16[2,1,2,64,512]{4,3,2,0,1:T(8,128)(2,1)S(1)}, bf16[2,1,2,64,512]{4,3,2,0,1:T(8,128)(2,1)S(1)}, u32[]{:S(2)}, u32[]{:S(2)}) collective-permute-start(bf16[2,1,2,64,512]{4,3,2,0,1:T(8,128)(2,1)S(1)} %get-tuple-element.1028), channel_id=1, source_target_pairs={{0,1},{1,2},{2,3},{3,4},{4,5},{5,6},{6,7},{8,9},{9,10},{10,11},{11... | collective-permute-start | bytes 786440 | tf_op jit(solution)/shard_map/while/body/eval_jaxpr/ppermute | solution.py:21
  545.9 52.2 %copy-start = (bf16[2,32,64,512]{3,2,1,0:T(8,128)(2,1)S(1)}, bf16[2,32,64,512]{3,2,1,0:T(8,128)(2,1)}, u32[]{:S(2)}) copy-start(bf16[2,32,64,512]{3,2,1,0:T(8,128)(2,1)} %fusion.186) | copy-start | bytes 12582916 | tf_op jit(solution)/shard_map/while
  545.9 52.2 %copy-start.1 = (bf16[1,32,64,512]{3,2,1,0:T(8,128)(2,1)S(1)}, bf16[1,32,64,512]{3,2,1,0:T(8,128)(2,1)}, u32[]{:S(2)}) copy-start(bf16[1,32,64,512]{3,2,1,0:T(8,128)(2,1)} %get-tuple-element.1025) | copy-start | bytes 6291460 | tf_op jit(solution)/shard_map/while
  550.9 90.8 %collective-permute-start.2 = (bf16[1,32,64,512]{3,2,1,0:T(8,128)(2,1)}, bf16[1,32,64,512]{3,2,1,0:T(8,128)(2,1)}, u32[]{:S(2)}, u32[]{:S(2)}) collective-permute-start(bf16[1,32,64,512]{3,2,1,0:T(8,128)(2,1)} %get-tuple-element.1054), channel_id=1, source_target_pairs={{8,0},{16,8},{24,16},{9,1},{17,9},{25,17},{10,2},{18,10},{26,18},{... | collective-permute-start | bytes 6291464 | tf_op jit(solution)/shard_map/while/body/eval_jaxpr/ppermute | solution.py:33
  552.3 91.2 %collective-permute-start.3 = (bf16[1,32,64,512]{3,2,1,0:T(8,128)(2,1)}, bf16[1,32,64,512]{3,2,1,0:T(8,128)(2,1)S(1)}, u32[]{:S(2)}, u32[]{:S(2)}) collective-permute-start(bf16[1,32,64,512]{3,2,1,0:T(8,128)(2,1)} %get-tuple-element.1055), channel_id=1, source_target_pairs={{0,8},{8,16},{16,24},{1,9},{9,17},{17,25},{2,10},{10,18},{18,26},{... | collective-permute-start | bytes 6291464 | tf_op jit(solution)/shard_map/while/body/eval_jaxpr/ppermute | solution.py:33
  710.5 110.6 %collective-permute-start = (bf16[2,1,2,64,512]{4,3,2,0,1:T(8,128)(2,1)S(1)}, bf16[2,1,2,64,512]{4,3,2,0,1:T(8,128)(2,1)S(1)}, u32[]{:S(2)}, u32[]{:S(2)}) collective-permute-start(bf16[2,1,2,64,512]{4,3,2,0,1:T(8,128)(2,1)S(1)} %get-tuple-element.1027), channel_id=1, source_target_pairs={{1,0},{2,1},{3,2},{4,3},{5,4},{6,5},{7,6},{9,8},{10,9},{11,10},{12... | collective-permute-start | bytes 786440 | tf_op jit(solution)/shard_map/while/body/eval_jaxpr/ppermute | solution.py:23
  711.8 109.3 %collective-permute-start.1 = (bf16[2,1,2,64,512]{4,3,2,0,1:T(8,128)(2,1)S(1)}, bf16[2,1,2,64,512]{4,3,2,0,1:T(8,128)(2,1)S(1)}, u32[]{:S(2)}, u32[]{:S(2)}) collective-permute-start(bf16[2,1,2,64,512]{4,3,2,0,1:T(8,128)(2,1)S(1)} %get-tuple-element.1028), channel_id=1, source_target_pairs={{0,1},{1,2},{2,3},{3,4},{4,5},{5,6},{6,7},{8,9},{9,10},{10,11},{11... | collective-permute-start | bytes 786440 | tf_op jit(solution)/shard_map/while/body/eval_jaxpr/ppermute | solution.py:21
  870.0 90.8 %collective-permute-start.2 = (bf16[1,32,64,512]{3,2,1,0:T(8,128)(2,1)}, bf16[1,32,64,512]{3,2,1,0:T(8,128)(2,1)}, u32[]{:S(2)}, u32[]{:S(2)}) collective-permute-start(bf16[1,32,64,512]{3,2,1,0:T(8,128)(2,1)} %get-tuple-element.1054), channel_id=1, source_target_pairs={{8,0},{16,8},{24,16},{9,1},{17,9},{25,17},{10,2},{18,10},{26,18},{... | collective-permute-start | bytes 6291464 | tf_op jit(solution)/shard_map/while/body/eval_jaxpr/ppermute | solution.py:33
  871.4 91.2 %collective-permute-start.3 = (bf16[1,32,64,512]{3,2,1,0:T(8,128)(2,1)}, bf16[1,32,64,512]{3,2,1,0:T(8,128)(2,1)S(1)}, u32[]{:S(2)}, u32[]{:S(2)}) collective-permute-start(bf16[1,32,64,512]{3,2,1,0:T(8,128)(2,1)} %get-tuple-element.1055), channel_id=1, source_target_pairs={{0,8},{8,16},{16,24},{1,9},{9,17},{17,25},{2,10},{10,18},{18,26},{... | collective-permute-start | bytes 6291464 | tf_op jit(solution)/shard_map/while/body/eval_jaxpr/ppermute | solution.py:33
  1029.6 110.6 %collective-permute-start = (bf16[2,1,2,64,512]{4,3,2,0,1:T(8,128)(2,1)S(1)}, bf16[2,1,2,64,512]{4,3,2,0,1:T(8,128)(2,1)S(1)}, u32[]{:S(2)}, u32[]{:S(2)}) collective-permute-start(bf16[2,1,2,64,512]{4,3,2,0,1:T(8,128)(2,1)S(1)} %get-tuple-element.1027), channel_id=1, source_target_pairs={{1,0},{2,1},{3,2},{4,3},{5,4},{6,5},{7,6},{9,8},{10,9},{11,10},{12... | collective-permute-start | bytes 786440 | tf_op jit(solution)/shard_map/while/body/eval_jaxpr/ppermute | solution.py:23
  1030.9 109.3 %collective-permute-start.1 = (bf16[2,1,2,64,512]{4,3,2,0,1:T(8,128)(2,1)S(1)}, bf16[2,1,2,64,512]{4,3,2,0,1:T(8,128)(2,1)S(1)}, u32[]{:S(2)}, u32[]{:S(2)}) collective-permute-start(bf16[2,1,2,64,512]{4,3,2,0,1:T(8,128)(2,1)S(1)} %get-tuple-element.1028), channel_id=1, source_target_pairs={{0,1},{1,2},{2,3},{3,4},{4,5},{5,6},{6,7},{8,9},{9,10},{10,11},{11... | collective-permute-start | bytes 786440 | tf_op jit(solution)/shard_map/while/body/eval_jaxpr/ppermute | solution.py:21
  1184.1 52.2 %copy-start = (bf16[2,32,64,512]{3,2,1,0:T(8,128)(2,1)S(1)}, bf16[2,32,64,512]{3,2,1,0:T(8,128)(2,1)}, u32[]{:S(2)}) copy-start(bf16[2,32,64,512]{3,2,1,0:T(8,128)(2,1)} %fusion.186) | copy-start | bytes 12582916 | tf_op jit(solution)/shard_map/while
  1184.1 52.2 %copy-start.1 = (bf16[1,32,64,512]{3,2,1,0:T(8,128)(2,1)S(1)}, bf16[1,32,64,512]{3,2,1,0:T(8,128)(2,1)}, u32[]{:S(2)}) copy-start(bf16[1,32,64,512]{3,2,1,0:T(8,128)(2,1)} %get-tuple-element.1025) | copy-start | bytes 6291460 | tf_op jit(solution)/shard_map/while
  1184.1 52.2 %copy-start.2 = (bf16[1,32,64,512]{3,2,1,0:T(8,128)(2,1)S(1)}, bf16[1,32,64,512]{3,2,1,0:T(8,128)(2,1)}, u32[]{:S(2)}) copy-start(bf16[1,32,64,512]{3,2,1,0:T(8,128)(2,1)} %get-tuple-element.1024) | copy-start | bytes 6291460 | tf_op jit(solution)/shard_map/while
  1189.1 90.8 %collective-permute-start.2 = (bf16[1,32,64,512]{3,2,1,0:T(8,128)(2,1)}, bf16[1,32,64,512]{3,2,1,0:T(8,128)(2,1)}, u32[]{:S(2)}, u32[]{:S(2)}) collective-permute-start(bf16[1,32,64,512]{3,2,1,0:T(8,128)(2,1)} %get-tuple-element.1054), channel_id=1, source_target_pairs={{8,0},{16,8},{24,16},{9,1},{17,9},{25,17},{10,2},{18,10},{26,18},{... | collective-permute-start | bytes 6291464 | tf_op jit(solution)/shard_map/while/body/eval_jaxpr/ppermute | solution.py:33
  1190.5 91.2 %collective-permute-start.3 = (bf16[1,32,64,512]{3,2,1,0:T(8,128)(2,1)}, bf16[1,32,64,512]{3,2,1,0:T(8,128)(2,1)S(1)}, u32[]{:S(2)}, u32[]{:S(2)}) collective-permute-start(bf16[1,32,64,512]{3,2,1,0:T(8,128)(2,1)} %get-tuple-element.1055), channel_id=1, source_target_pairs={{0,8},{8,16},{16,24},{1,9},{9,17},{17,25},{2,10},{10,18},{18,26},{... | collective-permute-start | bytes 6291464 | tf_op jit(solution)/shard_map/while/body/eval_jaxpr/ppermute | solution.py:33
  1348.8 110.6 %collective-permute-start = (bf16[2,1,2,64,512]{4,3,2,0,1:T(8,128)(2,1)S(1)}, bf16[2,1,2,64,512]{4,3,2,0,1:T(8,128)(2,1)S(1)}, u32[]{:S(2)}, u32[]{:S(2)}) collective-permute-start(bf16[2,1,2,64,512]{4,3,2,0,1:T(8,128)(2,1)S(1)} %get-tuple-element.1027), channel_id=1, source_target_pairs={{1,0},{2,1},{3,2},{4,3},{5,4},{6,5},{7,6},{9,8},{10,9},{11,10},{12... | collective-permute-start | bytes 786440 | tf_op jit(solution)/shard_map/while/body/eval_jaxpr/ppermute | solution.py:23
  1350.1 109.3 %collective-permute-start.1 = (bf16[2,1,2,64,512]{4,3,2,0,1:T(8,128)(2,1)S(1)}, bf16[2,1,2,64,512]{4,3,2,0,1:T(8,128)(2,1)S(1)}, u32[]{:S(2)}, u32[]{:S(2)}) collective-permute-start(bf16[2,1,2,64,512]{4,3,2,0,1:T(8,128)(2,1)S(1)} %get-tuple-element.1028), channel_id=1, source_target_pairs={{0,1},{1,2},{2,3},{3,4},{4,5},{5,6},{6,7},{8,9},{9,10},{10,11},{11... | collective-permute-start | bytes 786440 | tf_op jit(solution)/shard_map/while/body/eval_jaxpr/ppermute | solution.py:21
  1508.2 90.8 %collective-permute-start.2 = (bf16[1,32,64,512]{3,2,1,0:T(8,128)(2,1)}, bf16[1,32,64,512]{3,2,1,0:T(8,128)(2,1)}, u32[]{:S(2)}, u32[]{:S(2)}) collective-permute-start(bf16[1,32,64,512]{3,2,1,0:T(8,128)(2,1)} %get-tuple-element.1054), channel_id=1, source_target_pairs={{8,0},{16,8},{24,16},{9,1},{17,9},{25,17},{10,2},{18,10},{26,18},{... | collective-permute-start | bytes 6291464 | tf_op jit(solution)/shard_map/while/body/eval_jaxpr/ppermute | solution.py:33
  1509.7 91.2 %collective-permute-start.3 = (bf16[1,32,64,512]{3,2,1,0:T(8,128)(2,1)}, bf16[1,32,64,512]{3,2,1,0:T(8,128)(2,1)S(1)}, u32[]{:S(2)}, u32[]{:S(2)}) collective-permute-start(bf16[1,32,64,512]{3,2,1,0:T(8,128)(2,1)} %get-tuple-element.1055), channel_id=1, source_target_pairs={{0,8},{8,16},{16,24},{1,9},{9,17},{17,25},{2,10},{10,18},{18,26},{... | collective-permute-start | bytes 6291464 | tf_op jit(solution)/shard_map/while/body/eval_jaxpr/ppermute | solution.py:33
  1683.1 4.7 collective-permute-start.8
  1687.7 4.6 collective-permute-start.9
  (28 other events, 719.5 us)
Sparse Core Ops, SparseCore 0:
  1605.2 76.6 reduce-scatter.4
where the time goes:
time: 1720 us; the launch traced here: 1700 us
  other arithmetic  799 us (46%)
  local copies, waits for them, and re-layouts  338 us (20%)
  starting transfers between devices  229 us (13%)
  matrix products  151 us (9%)
  waiting for transfers between devices  139 us (8%)
  blocking collectives  27.1 us (2%)
    dot_general x5, other arithmetic, tick_step(): jnp.einsum('rbhwi,rbhwo->rio', depth, gated, preferred_element_type=jnp.f...  249 us
    gather x120, local copies, waits for them, and re-layouts  225 us
    reduce_sum x5, other arithmetic, tap_sums(): jnp.sum(back_mix.astype(jnp.float32) * window.astype(jnp.float32), axis=(...  214 us
    ppermute x10, starting transfers between devices, passed_along(): return lax.ppermute(shard, axis, pairs)  195 us
    while x15, other arithmetic  191 us
    dot_general x5, matrix products, tick_step(): jnp.einsum('rbhwo,rio->rbhwi', gated, weights[:, layer], preferred_elemen...  111 us
    ppermute x10, waiting for transfers between devices, passed_along(): return lax.ppermute(shard, axis, pairs)  75 us
    scatter x20, other arithmetic  68.5 us
  transfers between devices with their start and end apart: 27, of which 14 were waited for; matrix products, arithmetic and copies ran while one was open for 41% of the time, Pallas kernels for 0%

commit v1 on v0

v1 whole, which is shorter than its diff:
```python
import functools

import jax
import jax.numpy as jnp
import numpy as np
from jax import lax
from jax.experimental import pallas as pl
from jax.experimental.pallas import tpu as pltpu
from jax.sharding import PartitionSpec as P

H = 256
LANES = 128
CT = jnp.bfloat16
TILE = 16
ANY = pl.BlockSpec(memory_space=pl.ANY)
SMEM = pl.BlockSpec(memory_space=pltpu.SMEM)


def lane_block(block):
    return pl.ds(pl.multiple_of(block * LANES, LANES), LANES)


def shifted(value, offset, column):
    if offset == 0:
        return value
    cols = value.shape[0]
    turned = pltpu.roll(value, (-offset) % cols, 0)
    inside = column < cols - offset if offset > 0 else column >= -offset
    return jnp.where(inside, turned, 0.0)


def row_conv(source, row, lanes, taps, cols, column, sign):
    total = [None] * 5
    for row_tap in range(5):
        place = row + (row_tap if sign == 1 else 4 - row_tap)
        line = source[place, :, lanes].astype(CT).reshape(cols // TILE, TILE, LANES)
        for col_tap in range(5):
            term = line * taps[row_tap * 5 + col_tap, :, lanes][None]
            total[col_tap] = term if total[col_tap] is None else total[col_tap] + term
    out = None
    for col_tap in range(5):
        part = total[col_tap].reshape(cols, LANES).astype(jnp.float32)
        part = shifted(part, sign * (col_tap - 2), column)
        out = part if out is None else out + part
    return out


def spread_kernel(kern_ref, taps):
    channels = kern_ref.shape[1]
    for tap in range(25):
        taps[tap] = jnp.broadcast_to(kern_ref[tap : tap + 1, :].astype(CT), (TILE, channels))


def chain_kernel(replica, rows, cols, fresh, *refs):
    meta, recv, recv_top, recv_bot, entry, entry_top, entry_bot, masks, mask_top, mask_bot, weight, kern = refs[:12]
    refs = refs[12 if fresh else 15 :]
    sent, sent_top, sent_bot, outs, mixed, gates = refs[:6]
    up, seen, seen_halo, wbuf, kbuf, taps, bm, out, sems = refs[6:]
    channels = up.shape[2]
    micro = meta[1]

    @pl.when(meta[0] == 1)
    def _():
        loads = [
            pltpu.make_async_copy(masks.at[replica, 0, 0, micro, 0], seen, sems.at[0]),
            pltpu.make_async_copy(mask_top.at[replica, micro], seen_halo.at[pl.ds(0, 2)], sems.at[1]),
            pltpu.make_async_copy(mask_bot.at[replica, micro], seen_halo.at[pl.ds(2, 2)], sems.at[2]),
            pltpu.make_async_copy(weight.at[replica], wbuf, sems.at[3]),
            pltpu.make_async_copy(kern.at[replica], kbuf, sems.at[4]),
        ]
        for load in loads:
            load.start()

        def fetch(main, top, bot):
            pieces = [
                pltpu.make_async_copy(main, up.at[pl.ds(2, rows)], sems.at[5]),
                pltpu.make_async_copy(top, up.at[pl.ds(0, 2)], sems.at[6]),
                pltpu.make_async_copy(bot, up.at[pl.ds(rows + 2, 2)], sems.at[7]),
            ]
            for piece in pieces:
                piece.start()
            for piece in pieces:
                piece.wait()

        @pl.when(meta[2] == 1)
        def _():
            fetch(entry.at[replica, micro, 0], entry_top.at[replica, micro], entry_bot.at[replica, micro])

        @pl.when(meta[2] == 0)
        def _():
            fetch(recv, recv_top, recv_bot)

        for load in loads:
            load.wait()
        spread_kernel(kbuf, taps)
        for line in range(2):
            up[line] = up[line] * seen_halo[line]
            up[rows + 2 + line] = up[rows + 2 + line] * seen_halo[2 + line]

        @pl.loop(0, rows)
        def _(row):
            value = up[row + 2].astype(jnp.float32)
            up[row + 2] = jnp.where(seen[row] == 1, value, 0.0).astype(jnp.bfloat16)

        save_gates = pltpu.make_async_copy(up.at[pl.ds(2, rows)], gates.at[replica, micro], sems.at[0])
        save_gates.start()

        @pl.loop(0, (rows + 4) // 4)
        def _(part):
            lines = pl.ds(part * 4, 4)
            block = lax.dot_general(
                up[lines].reshape(4 * cols, channels),
                wbuf[...],
                (((1,), (1,)), ((), ())),
                preferred_element_type=jnp.float32,
            )
            bm[lines] = block.astype(jnp.bfloat16).reshape(4, cols, channels)

        save_mixed = pltpu.make_async_copy(bm.at[pl.ds(2, rows)], mixed.at[replica, micro], sems.at[1])
        save_mixed.start()
        column = lax.broadcasted_iota(jnp.int32, (cols, LANES), 0)

        @pl.loop(0, channels // LANES)
        def _(block):
            lanes = lane_block(block)

            @pl.loop(0, rows)
            def _(row):
                out[row, :, lanes] = row_conv(bm, row, lanes, taps, cols, column, -1).astype(jnp.bfloat16)

        stores = [
            pltpu.make_async_copy(out, sent, sems.at[2]),
            pltpu.make_async_copy(out.at[pl.ds(0, 2)], sent_top, sems.at[3]),
            pltpu.make_async_copy(out.at[pl.ds(rows - 2, 2)], sent_bot, sems.at[4]),
            pltpu.make_async_copy(out, outs.at[replica, micro], sems.at[5]),
        ]
        for store in stores:
            store.start()
        save_gates.wait()
        save_mixed.wait()
        for store in stores:
            store.wait()


def chain_step(replica, meta, recv, entry, masks, weight, kern, buffers):
    _, _, _, _, _, rows, cols, channels = masks[0].shape
    micro = masks[0].shape[3]
    fresh = buffers is None
    strip = jax.ShapeDtypeStruct((rows, cols, channels), jnp.bfloat16)
    edge = jax.ShapeDtypeStruct((2, cols, channels), jnp.bfloat16)
    whole = jax.ShapeDtypeStruct((2, micro, rows, cols, channels), jnp.bfloat16)
    operands = [meta, *recv, *entry, *masks, weight, kern]
    if not fresh:
        operands += list(buffers)
    results = pl.pallas_call(
        functools.partial(chain_kernel, replica, rows, cols, fresh),
        out_shape=(strip, edge, edge, whole, whole, whole),
        in_specs=[SMEM] + [ANY] * (len(operands) - 1),
        out_specs=(ANY,) * 6,
        scratch_shapes=[
            pltpu.VMEM((rows + 4, cols, channels), jnp.bfloat16),
            pltpu.VMEM((rows, cols, channels), jnp.int32),
            pltpu.VMEM((4, cols, channels), jnp.bfloat16),
            pltpu.VMEM((channels, channels), jnp.bfloat16),
            pltpu.VMEM((25, channels), jnp.float32),
            pltpu.VMEM((25, TILE, channels), CT),
            pltpu.VMEM((rows + 4, cols, channels), jnp.bfloat16),
            pltpu.VMEM((rows, cols, channels), jnp.bfloat16),
            pltpu.SemaphoreType.DMA((8,)),
        ],
        input_output_aliases={} if fresh else {12: 3, 13: 4, 14: 5},
        compiler_params=pltpu.CompilerParams(vmem_limit_bytes=40 << 20),
        cost_estimate=pl.CostEstimate(flops=60 * rows * cols * channels * 10, bytes_accessed=16 << 20, transcendentals=0),
    )(*operands)
    return results[:3], results[3:]


def grads_kernel(rows, cols, meta, acts, act_top, act_bot, kern, _mixed, _gates, wgrad, kgrad, mixed, gates, framed, kbuf, taps, bm, gated, depth, wsum, ksum, kout, sems):
    channels = framed.shape[2]
    replica = meta[0]
    micro = meta[1]
    loads = [
        pltpu.make_async_copy(acts.at[replica, 0, 0, micro, 0], framed.at[pl.ds(2, rows)], sems.at[0]),
        pltpu.make_async_copy(act_top.at[replica, micro], framed.at[pl.ds(0, 2)], sems.at[1]),
        pltpu.make_async_copy(act_bot.at[replica, micro], framed.at[pl.ds(rows + 2, 2)], sems.at[2]),
        pltpu.make_async_copy(kern.at[replica], kbuf, sems.at[3]),
        pltpu.make_async_copy(mixed.at[replica, micro], bm, sems.at[4]),
        pltpu.make_async_copy(gates.at[replica, micro], gated, sems.at[5]),
    ]
    for load in loads:
        load.start()
    for load in loads:
        load.wait()
    spread_kernel(kbuf, taps)
    column = lax.broadcasted_iota(jnp.int32, (cols, LANES), 0)
    ksum[...] = jnp.zeros_like(ksum)

    @pl.loop(0, channels // LANES)
    def _(block):
        lanes = lane_block(block)

        @pl.loop(0, rows)
        def _(row):
            depth[row, :, lanes] = row_conv(framed, row, lanes, taps, cols, column, 1).astype(jnp.bfloat16)

        @pl.loop(0, rows)
        def _(row):
            wide = bm[row, :, lanes].astype(jnp.float32)
            for col_tap in range(5):
                moved = shifted(wide, 2 - col_tap, column).astype(CT).reshape(cols // TILE, TILE, LANES)
                for row_tap in range(5):
                    line = framed[row + row_tap, :, lanes].astype(CT).reshape(cols // TILE, TILE, LANES)
                    part = moved * line
                    short = part[0]
                    for piece in range(1, cols // TILE):
                        short = short + part[piece]
                    short = short.astype(jnp.float32).reshape(TILE // 8, 8, LANES)
                    tap = row_tap * 5 + col_tap
                    ksum[tap, :, lanes] = ksum[tap, :, lanes] + jnp.sum(short, axis=0)

    wsum[...] = jnp.zeros_like(wsum)

    @pl.loop(0, rows // 8)
    def _(part):
        lines = pl.ds(part * 8, 8)
        wsum[...] += lax.dot_general(
            depth[lines].reshape(8 * cols, channels),
            gated[lines].reshape(8 * cols, channels),
            (((0,), (0,)), ((), ())),
            preferred_element_type=jnp.float32,
        )

    kout[...] = jnp.sum(ksum[...], axis=1)
    stores = [
        pltpu.make_async_copy(wsum, wgrad, sems.at[0]),
        pltpu.make_async_copy(kout, kgrad, sems.at[1]),
    ]
    for store in stores:
        store.start()
    for store in stores:
        store.wait()


def grads_step(meta, acts, kern, mixed, gates):
    _, _, _, micro, _, rows, cols, channels = acts[0].shape
    strip = pltpu.VMEM((rows, cols, channels), jnp.bfloat16)
    whole = jax.ShapeDtypeStruct((2, micro, rows, cols, channels), jnp.bfloat16)
    return pl.pallas_call(
        functools.partial(grads_kernel, rows, cols),
        out_shape=(
            jax.ShapeDtypeStruct((channels, channels), jnp.float32),
            jax.ShapeDtypeStruct((25, channels), jnp.float32),
            whole,
            whole,
        ),
        in_specs=[SMEM] + [ANY] * 6,
        out_specs=(ANY,) * 4,
        scratch_shapes=[
            pltpu.VMEM((rows + 4, cols, channels), jnp.bfloat16),
            pltpu.VMEM((25, channels), jnp.float32),
            pltpu.VMEM((25, TILE, channels), CT),
            strip,
            strip,
            strip,
            pltpu.VMEM((channels, channels), jnp.float32),
            pltpu.VMEM((25, 8, channels), jnp.float32),
            pltpu.VMEM((25, channels), jnp.float32),
            pltpu.SemaphoreType.DMA((6,)),
        ],
        input_output_aliases={5: 2, 6: 3},
        compiler_params=pltpu.CompilerParams(vmem_limit_bytes=40 << 20),
        cost_estimate=pl.CostEstimate(flops=120 * rows * cols * channels * 10, bytes_accessed=8 << 20, transcendentals=0),
    )(meta, *acts, kern, mixed, gates)


def edges(cells, dim):
    count = lax.axis_size("strip")
    size = cells.shape[dim]
    head = lax.slice_in_dim(cells, 0, 2, axis=dim)
    tail = lax.slice_in_dim(cells, size - 2, size, axis=dim)
    above = lax.ppermute(tail, "strip", [(i, i + 1) for i in range(count - 1)])
    below = lax.ppermute(head, "strip", [(i + 1, i) for i in range(count - 1)])
    return above, below


def passed_along(values, by, sources):
    main, head, tail = values
    count = lax.axis_size("strip")
    axes = ("sec", "strip")
    above = lax.ppermute(
        tail, axes, [(p * count + z, (p + by) * count + z + 1) for p in sources for z in range(count - 1)]
    )
    below = lax.ppermute(
        head, axes, [(p * count + z + 1, (p + by) * count + z) for p in sources for z in range(count - 1)]
    )
    main = lax.ppermute(main, "sec", [(p, p + by) for p in sources])
    return main, above, below


def timetable(sections, micro):
    order = []
    for p in range(sections):
        runs = [(m + sections - 1 - p, 0, m) for m in range(micro)] + [(m + p, 1, m) for m in range(micro)]
        order.append(sorted(runs))
    ready = [max(order[p][k][0] for p in range(sections)) for k in range(2 * micro)]
    table = np.array([[run[1:] for run in runs] for runs in order], np.int32)
    return table, ready


def body(activations, relu_masks, grad_in, mix_weight, depth_kernel):
    sections = lax.axis_size("sec")
    position = lax.axis_index("sec")
    micro = activations.shape[3]
    rows, cols, channels = activations.shape[5:]
    mirror = [(i, sections - 1 - i) for i in range(sections)]

    mask_ends = jnp.concatenate([relu_masks[:, 0, 0, :, 0, :2], relu_masks[:, 0, 0, :, 0, -2:]], axis=2)
    mask_ends = (mask_ends == 1).astype(jnp.bfloat16)
    grad_ends = jnp.concatenate([grad_in[:, :, 0, :2], grad_in[:, :, 0, -2:]], axis=2)
    first = edges(jnp.stack([mask_ends, grad_ends]), 3)
    mask_top, grad_top = first[0][0], first[0][1]
    mask_bot, grad_bot = first[1][0], first[1][1]
    packed = jnp.concatenate([mix_weight[0, 0], depth_kernel[0, 0]], axis=0)
    mirrored = lax.ppermute(packed, "sec", mirror)
    weights = jnp.stack([mix_weight[0, 0], mirrored[:channels]])
    kernels = jnp.stack([depth_kernel[0, 0], mirrored[channels:]]).astype(jnp.float32)
    act_top, act_bot = edges(activations[:, 0, 0, :, 0], 2)

    masks = (relu_masks, mask_top, mask_bot)
    entry = (grad_in, grad_top, grad_bot)
    acts = (activations, act_top, act_bot)
    table, ready = timetable(sections, micro)
    table = jnp.asarray(table)[position]

    edge = jnp.zeros((2, cols, channels), jnp.bfloat16)
    nothing = (jnp.zeros((rows, cols, channels), jnp.bfloat16), edge, edge)
    received = [nothing, nothing]
    buffers = None
    grads_w = [0.0, 0.0]
    grads_k = [0.0, 0.0]
    ticks = micro + sections - 1
    for tick in range(ticks):
        waiting = received
        received = [None, None]
        for replica in range(2):
            depth_in = sections - 1 - position if replica == 0 else position
            wanted = tick - depth_in
            valid = (wanted >= 0) & (wanted < micro)
            meta = jnp.stack([valid, jnp.clip(wanted, 0, micro - 1), depth_in == 0]).astype(jnp.int32)
            values, buffers = chain_step(
                replica, meta, waiting[replica], entry, masks, weights, kernels, buffers
            )
            if tick < ticks - 1:
                by = -1 if replica == 0 else 1
                sources = [
                    p
                    for p in range(sections)
                    if 0 <= p + by < sections
                    and 0 <= tick - (sections - 1 - p if replica == 0 else p) < micro
                ]
                received[replica] = passed_along(values, by, sources)
        for k in range(2 * micro):
            if ready[k] != tick:
                continue
            run = table[k]
            outs, mixed, gates = buffers
            wgrad, kgrad, mixed, gates = grads_step(run, acts, kernels, mixed, gates)
            buffers = (outs, mixed, gates)
            for replica in range(2):
                mine = run[0] == replica
                grads_w[replica] = grads_w[replica] + jnp.where(mine, wgrad, 0.0)
                grads_k[replica] = grads_k[replica] + jnp.where(mine, kgrad, 0.0)

    factor = 1.0 / H
    both_w = jnp.concatenate(grads_w, axis=1).astype(jnp.bfloat16)
    shares = lax.psum_scatter(both_w, "strip", scatter_dimension=0, tiled=True).astype(jnp.float32)
    kernel_all = lax.psum(jnp.stack(grads_k).astype(jnp.bfloat16), "strip").astype(jnp.float32)
    share_rows = shares.shape[0]
    partner = jnp.concatenate([shares[:, channels:], kernel_all[1]], axis=0).astype(jnp.bfloat16)
    partner = lax.ppermute(partner, "sec", mirror).astype(jnp.float32)
    share_w = (shares[:, :channels] + partner[:share_rows]) * factor
    full_k = (kernel_all[0] + partner[share_rows:]) * factor
    return buffers[0][:, None, :, None], share_w[None, None], full_k[None, None]


def solution(mesh):
    placed = (
        P(None, "sec", None, None, None, "strip", None, None),
        P(None, "sec", None, None, None, "strip", None, None),
        P(None, None, None, "strip", None, None),
        P("sec", None, None, None),
        P("sec", None, None, None),
    )
    return jax.shard_map(
        body,
        mesh=mesh,
        in_specs=placed,
        out_specs=(
            P(None, "sec", None, None, "strip", None, None),
            P("sec", None, "strip", None),
            P("sec", None, None, None),
        ),
        check_vma=False,
    )
```

time: 1720 us -> 568 us (0.33); the launches traced: 1700 us -> 567 us
  other arithmetic: 799 us -> 8.95 us
  local copies, waits for them, and re-layouts: 338 us -> 42.6 us
  Pallas kernels: 0 us -> 174 us
  starting transfers between devices: 229 us -> 59.3 us
  matrix products: 151 us -> 0 us
  blocking collectives: 27.1 us -> 90.4 us
  waiting for transfers between devices: 139 us -> 171 us
    dot_general x5 -> x0, other arithmetic: 249 us -> none  [tick_step(): jnp.einsum('rbhwi,rbhwo->rio', depth, gated, preferred_element_type=jnp.f...]
    gather x125 -> x0, local copies, waits for them, and re-layouts: 225 us -> none
    reduce_sum x5 -> x0, other arithmetic: 214 us -> none  [tap_sums(): jnp.sum(back_mix.astype(jnp.float32) * window.astype(jnp.float32), axis=(...]
    while x15 -> x0, other arithmetic: 191 us -> none
    pallas_call x0 -> x14, Pallas kernels: none -> 174 us  [the longest x4 91.2 us: grads_step(): pl.pallas_call(functools.partial(grads_kernel, rows, cols), out_shape=(ja...]
    ppermute x26 -> x30, starting transfers between devices: 229 us -> 59.2 us  [the longest x8 27.3 us: passed_along(): main = lax.ppermute(main, 'sec', [(p, p + by) for p in sources])]
    dot_general x10 -> x0, matrix products: 151 us -> none  [the longest x5 111 us: tick_step(): jnp.einsum('rbhwo,rio->rbhwi', gated, weights[:, layer], preferred_elemen...]
    ppermute x26 -> x30, waiting for transfers between devices: 89.5 us -> 167 us  [the longest x8 114 us: passed_along(): lax.ppermute(head, axes, [(p * count + z + 1, (p + by) * count + z) for p...]
  transfers between devices with their start and end apart: 27 -> 31, of which waited for: 14 -> 7; matrix products, arithmetic and copies ran while one was open for 41% -> 2% of each run, Pallas kernels for 0% -> 26%
where the time goes in v1:
time: 568 us; the launch traced here: 567 us
  Pallas kernels  174 us (31%)
  waiting for transfers between devices  171 us (30%)
  blocking collectives  90.4 us (16%)
  starting transfers between devices  59.3 us (10%)
  local copies, waits for them, and re-layouts  42.6 us (8%)
  between operations  20.1 us (4%)
  other arithmetic  8.95 us (2%)
    ppermute x8, waiting for transfers between devices, passed_along(): lax.ppermute(head, axes, [(p * count + z + 1, (p + by) * count + z) for p...  114 us
    pallas_call x4, Pallas kernels, grads_step(): pl.pallas_call(functools.partial(grads_kernel, rows, cols), out_shape=(ja...  91.2 us
    psum x1, blocking collectives, body(): lax.psum(jnp.stack(grads_k).astype(jnp.bfloat16), 'strip')  90.4 us
    pallas_call x10, Pallas kernels, chain_step(): pl.pallas_call(functools.partial(chain_kernel, replica, rows, cols, fresh...  82.7 us
    ppermute x8, waiting for transfers between devices, passed_along(): lax.ppermute(tail, axes, [(p * count + z, (p + by) * count + z + 1) for p...  33.4 us
    unnamed x63, local copies, waits for them, and re-layouts  31.7 us
    ppermute x8, starting transfers between devices, passed_along(): main = lax.ppermute(main, 'sec', [(p, p + by) for p in sources])  27.3 us
    ppermute x8, starting transfers between devices, passed_along(): lax.ppermute(tail, axes, [(p * count + z, (p + by) * count + z + 1) for p...  13.3 us
  transfers between devices with their start and end apart: 31, of which 7 were waited for; matrix products, arithmetic and copies ran while one was open for 2% of the time, Pallas kernels for 26%

profile of v1, /device:TPU:0, one launch (start us, length us, event | category | flops | bytes accessed | tf_op | source)
XLA Modules:
  0.0 566.7 jit_solution(8533450166658142950)
XLA Ops:
  9.1 3.9 collective-permute-start.2
  20.9 5.0 collective-permute-done.2
  31.9 2.1 collective-permute-start.6
  34.0 19.7 %shard_map.86 = (bf16[32,64,512]{2,1,0:T(8,128)(2,1)}, bf16[2,64,512]{2,1,0:T(8,128)(2,1)S(1)}, bf16[2,64,512]{2,1,0:T(8,128)(2,1)S(1)}, bf16[2,2,32,64,512]{4,3...) custom-call(s32[3]{0:T(128)S(1)} %get-tuple-element.166.refs_0_, ...), custom_call_target="tpu_custom_call", output_to_operand_aliasing={{3}: (12, {}), {4}: (13, {}), {5}: (14, {})} | custom-call | flops 629145600 | bytes 16777216 | tf_op jit(solution)/shard_map/pallas_call | solution.py:155
  55.0 2.6 collective-permute-start.3
  63.0 2.1 collective-permute-start.12
  65.1 33.4 %collective-permute-done.4.refs_2_ = bf16[2,64,512]{2,1,0:T(8,128)(2,1)S(1)} collective-permute-done((bf16[2,64,512]{2,1,0:T(8,128)(2,1)}, bf16[2,64,512]{2,1,0:T(8,128)(2,1)S(1)}, u32[]{:S(2)}, u32[]{:S(2)}) %collective-permute-start.4) | collective-permute-done | bytes 131104 | tf_op jit(solution)/shard_map/ppermute | solution.py:290
  98.5 19.7 %shard_map.88 = (bf16[32,64,512]{2,1,0:T(8,128)(2,1)}, bf16[2,64,512]{2,1,0:T(8,128)(2,1)S(1)}, bf16[2,64,512]{2,1,0:T(8,128)(2,1)S(1)}, bf16[2,2,32,64,512]{4,3...) custom-call(s32[3]{0:T(128)S(1)} %add_add_fusion.3.refs_0_, ...), custom_call_target="tpu_custom_call", output_to_operand_aliasing={{3}: (12, {}), {4}: (13, {}), {5}: (14, {})} | custom-call | flops 629145600 | bytes 16777216 | tf_op jit(solution)/shard_map/pallas_call | solution.py:155
  119.5 14.0 %collective-permute-start.9 = (bf16[32,64,512]{2,1,0:T(8,128)(2,1)}, bf16[32,64,512]{2,1,0:T(8,128)(2,1)}, u32[]{:S(2)}, u32[]{:S(2)}) collective-permute-start(bf16[32,64,512]{2,1,0:T(8,128)(2,1)} %get-tuple-element.86), channel_id=1, source_target_pairs={{0,8},{8,16},{1,9},{9,17},{2,10},{10,18},{3,11},{11,19},{4,12},{12... | collective-permute-start | bytes 6291464 | tf_op jit(solution)/shard_map/ppermute | solution.py:296
  133.4 2.3 fusion.8
  135.7 2.1 collective-permute-start.15
  141.3 10.1 %collective-permute-done.16.act_bot = bf16[2,2,2,64,512]{4,3,2,1,0:T(8,128)(2,1)} collective-permute-done((bf16[2,2,2,64,512]{4,3,2,1,0:T(8,128)(2,1)}, bf16[2,2,2,64,512]{4,3,2,1,0:T(8,128)(2,1)}, u32[]{:S(2)}, u32[]{:S(2)}) %collective-permute-start.16) | collective-permute-done | bytes 524320 | tf_op jit(solution)/shard_map/ppermute | solution.py:282
  151.4 8.1 %collective-permute-start.10 = (bf16[2,64,512]{2,1,0:T(8,128)(2,1)}, bf16[2,64,512]{2,1,0:T(8,128)(2,1)S(1)}, u32[]{:S(2)}, u32[]{:S(2)}) collective-permute-start(bf16[2,64,512]{2,1,0:T(8,128)(2,1)} %copy-done.15), channel_id=1, source_target_pairs={{0,9},{1,10},{2,11},{3,12},{4,13},{5,14},{6,15},{8,17},{9,18},{10,... | collective-permute-start | bytes 393224 | tf_op jit(solution)/shard_map/ppermute | solution.py:290
  160.2 3.4 copy-done
  163.6 22.8 %shard_map.89 = (f32[512,512]{1,0:T(8,128)S(1)}, f32[25,512]{1,0:T(8,128)S(1)}, bf16[2,2,32,64,512]{4,3,2,1,0:T(8,128)(2,1)S(1)}, bf16[2,2,32,64,512]{4,3,2,1,0:T(8,128)(2,1)}) custom-call(s32[2]{0:T(128)S(1)} %get-tuple-element.165.meta, bf16[2,1,1,2,1,32,64,512]{7,6,5,4,3,2,1,0:T(8,128)(2,1)} %acts.7, ...), custom_call_target="tpu_custom_call", output_to_operand_aliasing={{2}: (5, {}), {3}: (6, {})} | custom-call | flops 1258291200 | bytes 8388608 | tf_op jit(solution)/shard_map/pallas_call | solution.py:248
  186.4 3.3 copy-done.1
  199.5 3.4 copy-done.2
  202.9 22.8 %shard_map.92 = (f32[512,512]{1,0:T(8,128)S(1)}, f32[25,512]{1,0:T(8,128)S(1)}, bf16[2,2,32,64,512]{4,3,2,1,0:T(8,128)(2,1)S(1)}, bf16[2,2,32,64,512]{4,3,2,1,0:T(8,128)(2,1)}) custom-call(s32[2]{0:T(128)S(1)} %get-tuple-element.164.meta, bf16[2,1,1,2,1,32,64,512]{7,6,5,4,3,2,1,0:T(8,128)(2,1)} %acts.7, ...), custom_call_target="tpu_custom_call", output_to_operand_aliasing={{2}: (5, {}), {3}: (6, {})} | custom-call | flops 1258291200 | bytes 8388608 | tf_op jit(solution)/shard_map/pallas_call | solution.py:248
  225.7 3.3 copy-done.3
  229.0 79.9 %collective-permute-done.22.refs_3_ = bf16[2,64,512]{2,1,0:T(8,128)(2,1)S(1)} collective-permute-done((bf16[2,64,512]{2,1,0:T(8,128)(2,1)}, bf16[2,64,512]{2,1,0:T(8,128)(2,1)S(1)}, u32[]{:S(2)}, u32[]{:S(2)}) %collective-permute-start.22) | collective-permute-done | bytes 131104 | tf_op jit(solution)/shard_map/ppermute | solution.py:293
  308.9 19.7 %shard_map.93 = (bf16[32,64,512]{2,1,0:T(8,128)(2,1)}, bf16[2,64,512]{2,1,0:T(8,128)(2,1)S(1)}, bf16[2,64,512]{2,1,0:T(8,128)(2,1)S(1)}, bf16[2,2,32,64,512]{4,3...) custom-call(s32[3]{0:T(128)S(1)} %add_add_fusion.8.refs_0_, ...), custom_call_target="tpu_custom_call", output_to_operand_aliasing={{3}: (12, {}), {4}: (13, {}), {5}: (14, {})} | custom-call | flops 629145600 | bytes 16777216 | tf_op jit(solution)/shard_map/pallas_call | solution.py:155
  331.9 2.0 collective-permute-start.23
  343.3 3.4 copy-done.4
  346.6 22.8 %shard_map.95 = (f32[512,512]{1,0:T(8,128)S(1)}, f32[25,512]{1,0:T(8,128)S(1)}, bf16[2,2,32,64,512]{4,3,2,1,0:T(8,128)(2,1)S(1)}, bf16[2,2,32,64,512]{4,3,2,1,0:T(8,128)(2,1)}) custom-call(s32[2]{0:T(128)S(1)} %get-tuple-element.163.meta, bf16[2,1,1,2,1,32,64,512]{7,6,5,4,3,2,1,0:T(8,128)(2,1)} %acts.7, ...), custom_call_target="tpu_custom_call", output_to_operand_aliasing={{2}: (5, {}), {3}: (6, {})} | custom-call | flops 1258291200 | bytes 8388608 | tf_op jit(solution)/shard_map/pallas_call | solution.py:248
  369.4 3.3 copy-done.5
  372.8 34.6 %collective-permute-done.28.refs_3_ = bf16[2,64,512]{2,1,0:T(8,128)(2,1)S(1)} collective-permute-done((bf16[2,64,512]{2,1,0:T(8,128)(2,1)}, bf16[2,64,512]{2,1,0:T(8,128)(2,1)S(1)}, u32[]{:S(2)}, u32[]{:S(2)}) %collective-permute-start.28) | collective-permute-done | bytes 131104 | tf_op jit(solution)/shard_map/ppermute | solution.py:293
  407.3 19.8 %shard_map.96 = (bf16[32,64,512]{2,1,0:T(8,128)(2,1)}, bf16[2,64,512]{2,1,0:T(8,128)(2,1)}, bf16[2,64,512]{2,1,0:T(8,128)(2,1)}, bf16[2,2,32,64,512]{4,3,2,1,0:T...) custom-call(s32[3]{0:T(128)S(1)} %add_add_fusion.9.refs_0_, ...), custom_call_target="tpu_custom_call", output_to_operand_aliasing={{3}: (12, {}), {4}: (13, {}), {5}: (14, {})} | custom-call | flops 629145600 | bytes 16777216 | tf_op jit(solution)/shard_map/pallas_call | solution.py:155
  427.8 3.4 copy-done.6
  431.2 22.8 %shard_map.98 = (f32[512,512]{1,0:T(8,128)S(1)}, f32[25,512]{1,0:T(8,128)S(1)}, bf16[2,2,32,64,512]{4,3,2,1,0:T(8,128)(2,1)S(1)}, bf16[2,2,32,64,512]{4,3,2,1,0:T(8,128)(2,1)}) custom-call(s32[2]{0:T(128)S(1)} %get-tuple-element.162.meta, bf16[2,1,1,2,1,32,64,512]{7,6,5,4,3,2,1,0:T(8,128)(2,1)} %acts.7, ...), custom_call_target="tpu_custom_call", output_to_operand_aliasing={{2}: (5, {}), {3}: (6, {})} | custom-call | flops 1258291200 | bytes 8388608 | tf_op jit(solution)/shard_map/pallas_call | solution.py:248
  455.9 90.4 %psum.7 = bf16[2,25,512]{2,1,0:T(8,128)(2,1)S(1)} all-reduce(bf16[2,25,512]{2,1,0:T(8,128)(2,1)S(1)} %pad_maximum_fusion.5), channel_id=1, replica_groups=mesh['sec'=4,'strip'=8] {'strip'}, use_global_device_ids=true, to_apply=%region_1.2 | all-reduce | flops 25600 | bytes 102400 | tf_op jit(solution)/shard_map/psum | solution.py:377
  546.3 4.8 reduce-scatter.2.cloned.1.call-done
  554.0 3.6 collective-permute-done.29
  (146 shorter events, 52.2 us)
Async XLA Ops:
  7.2 544.0 %reduce-scatter.2.cloned.1.call-start = ((), (), s32[]{:S(2)}) async-start(), calls=%async_computation.1 | async-start | bytes 1179648 | tf_op jit(solution)/shard_map/reduce_scatter | solution.py:376
  9.1 16.8 %collective-permute-start.2 = (bf16[537,512]{1,0:T(8,128)(2,1)}, bf16[537,512]{1,0:T(8,128)(2,1)}, u32[]{:S(2)}, u32[]{:S(2)}) collective-permute-start(bf16[537,512]{1,0:T(8,128)(2,1)} %pad_maximum_fusion.3), channel_id=1, source_target_pairs={{0,24},{8,16},{16,8},{24,0},{1,25},{9,17},{17,9},{25,1},{2,26},{10... | collective-permute-start | bytes 1649672 | tf_op jit(solution)/shard_map/ppermute | solution.py:324
  18.0 11.0 %collective-permute-start = (bf16[2,2,2,2,64,512]{5,4,3,2,1,0:T(8,128)(2,1)}, bf16[2,2,2,2,64,512]{5,4,3,2,1,0:T(8,128)(2,1)S(1)}, u32[]{:S(2)}, u32[]{:S(2)}) collective-permute-start(bf16[2,2,2,2,64,512]{5,4,3,2,1,0:T(8,128)(2,1)} %get-tuple-element.151), channel_id=1, source_target_pairs={{0,1},{1,2},{2,3},{3,4},{4,5},{5,6},{6,7},{8,9},{9,10},{10,11},{11... | collective-permute-start | bytes 3145736 | tf_op jit(solution)/shard_map/ppermute | solution.py:281
  19.5 9.5 %collective-permute-start.1 = (bf16[2,2,2,2,64,512]{5,4,3,2,1,0:T(8,128)(2,1)}, bf16[2,2,2,2,64,512]{5,4,3,2,1,0:T(8,128)(2,1)}, u32[]{:S(2)}, u32[]{:S(2)}) collective-permute-start(bf16[2,2,2,2,64,512]{5,4,3,2,1,0:T(8,128)(2,1)} %get-tuple-element.150), channel_id=1, source_target_pairs={{1,0},{2,1},{3,2},{4,3},{5,4},{6,5},{7,6},{9,8},{10,9},{11,10},{12... | collective-permute-start | bytes 3145736 | tf_op jit(solution)/shard_map/ppermute | solution.py:282
  31.9 29.2 %collective-permute-start.6 = (bf16[32,64,512]{2,1,0:T(8,128)(2,1)}, bf16[32,64,512]{2,1,0:T(8,128)(2,1)}, u32[]{:S(2)}, u32[]{:S(2)}) collective-permute-start(bf16[32,64,512]{2,1,0:T(8,128)(2,1)} %get-tuple-element.77), channel_id=1, source_target_pairs={{24,16},{25,17},{26,18},{27,19},{28,20},{29,21},{30,22},{31,23}} | collective-permute-start | bytes 6291464 | tf_op jit(solution)/shard_map/ppermute | solution.py:296
  55.0 43.5 %collective-permute-start.3 = (bf16[32,64,512]{2,1,0:T(8,128)(2,1)}, bf16[32,64,512]{2,1,0:T(8,128)(2,1)}, u32[]{:S(2)}, u32[]{:S(2)}) collective-permute-start(bf16[32,64,512]{2,1,0:T(8,128)(2,1)} %get-tuple-element.74), channel_id=1, source_target_pairs={{0,8},{1,9},{2,10},{3,11},{4,12},{5,13},{6,14},{7,15}} | collective-permute-start | bytes 6291464 | tf_op jit(solution)/shard_map/ppermute | solution.py:296
  57.6 2.7 collective-permute-start.7
  58.3 2.8 collective-permute-start.8
  59.0 39.4 %collective-permute-start.4 = (bf16[2,64,512]{2,1,0:T(8,128)(2,1)}, bf16[2,64,512]{2,1,0:T(8,128)(2,1)S(1)}, u32[]{:S(2)}, u32[]{:S(2)}) collective-permute-start(bf16[2,64,512]{2,1,0:T(8,128)(2,1)} %copy-done.25), channel_id=1, source_target_pairs={{0,9},{1,10},{2,11},{3,12},{4,13},{5,14},{6,15}} | collective-permute-start | bytes 393224 | tf_op jit(solution)/shard_map/ppermute | solution.py:290
  60.3 38.1 %collective-permute-start.5 = (bf16[2,64,512]{2,1,0:T(8,128)(2,1)}, bf16[2,64,512]{2,1,0:T(8,128)(2,1)S(1)}, u32[]{:S(2)}, u32[]{:S(2)}) collective-permute-start(bf16[2,64,512]{2,1,0:T(8,128)(2,1)} %copy-done.24), channel_id=1, source_target_pairs={{1,8},{2,9},{3,10},{4,11},{5,12},{6,13},{7,14}} | collective-permute-start | bytes 393224 | tf_op jit(solution)/shard_map/ppermute | solution.py:293
  63.0 126.7 %collective-permute-start.12 = (bf16[32,64,512]{2,1,0:T(8,128)(2,1)}, bf16[32,64,512]{2,1,0:T(8,128)(2,1)}, u32[]{:S(2)}, u32[]{:S(2)}) collective-permute-start(bf16[32,64,512]{2,1,0:T(8,128)(2,1)} %get-tuple-element.89), channel_id=1, source_target_pairs={{16,8},{24,16},{17,9},{25,17},{18,10},{26,18},{19,11},{27,19},{20,... | collective-permute-start | bytes 6291464 | tf_op jit(solution)/shard_map/ppermute | solution.py:296
  119.5 72.6 %collective-permute-start.9 = (bf16[32,64,512]{2,1,0:T(8,128)(2,1)}, bf16[32,64,512]{2,1,0:T(8,128)(2,1)}, u32[]{:S(2)}, u32[]{:S(2)}) collective-permute-start(bf16[32,64,512]{2,1,0:T(8,128)(2,1)} %get-tuple-element.86), channel_id=1, source_target_pairs={{0,8},{8,16},{1,9},{9,17},{2,10},{10,18},{3,11},{11,19},{4,12},{12... | collective-permute-start | bytes 6291464 | tf_op jit(solution)/shard_map/ppermute | solution.py:296
  135.7 4.9 collective-permute-start.15
  137.8 13.6 %collective-permute-start.16 = (bf16[2,2,2,64,512]{4,3,2,1,0:T(8,128)(2,1)}, bf16[2,2,2,64,512]{4,3,2,1,0:T(8,128)(2,1)}, u32[]{:S(2)}, u32[]{:S(2)}) collective-permute-start(bf16[2,2,2,64,512]{4,3,2,1,0:T(8,128)(2,1)} %get-tuple-element.144), channel_id=1, source_target_pairs={{1,0},{2,1},{3,2},{4,3},{5,4},{6,5},{7,6},{9,8},{10,9},{11,10},{12... | collective-permute-start | bytes 1572872 | tf_op jit(solution)/shard_map/ppermute | solution.py:282
  139.8 19.7 %collective-permute-start.13 = (bf16[2,64,512]{2,1,0:T(8,128)(2,1)}, bf16[2,64,512]{2,1,0:T(8,128)(2,1)S(1)}, u32[]{:S(2)}, u32[]{:S(2)}) collective-permute-start(bf16[2,64,512]{2,1,0:T(8,128)(2,1)} %copy-done.19), channel_id=1, source_target_pairs={{16,9},{17,10},{18,11},{19,12},{20,13},{21,14},{22,15},{24,17},{25... | collective-permute-start | bytes 393224 | tf_op jit(solution)/shard_map/ppermute | solution.py:290
  140.6 49.2 %collective-permute-start.14 = (bf16[2,64,512]{2,1,0:T(8,128)(2,1)}, bf16[2,64,512]{2,1,0:T(8,128)(2,1)S(1)}, u32[]{:S(2)}, u32[]{:S(2)}) collective-permute-start(bf16[2,64,512]{2,1,0:T(8,128)(2,1)} %copy-done.14), channel_id=1, source_target_pairs={{17,8},{18,9},{19,10},{20,11},{21,12},{22,13},{23,14},{25,16},{26,... | collective-permute-start | bytes 393224 | tf_op jit(solution)/shard_map/ppermute | solution.py:293
  151.4 40.6 %collective-permute-start.10 = (bf16[2,64,512]{2,1,0:T(8,128)(2,1)}, bf16[2,64,512]{2,1,0:T(8,128)(2,1)S(1)}, u32[]{:S(2)}, u32[]{:S(2)}) collective-permute-start(bf16[2,64,512]{2,1,0:T(8,128)(2,1)} %copy-done.15), channel_id=1, source_target_pairs={{0,9},{1,10},{2,11},{3,12},{4,13},{5,14},{6,15},{8,17},{9,18},{10,... | collective-permute-start | bytes 393224 | tf_op jit(solution)/shard_map/ppermute | solution.py:290
  159.6 32.5 %collective-permute-start.11 = (bf16[2,64,512]{2,1,0:T(8,128)(2,1)}, bf16[2,64,512]{2,1,0:T(8,128)(2,1)S(1)}, u32[]{:S(2)}, u32[]{:S(2)}) collective-permute-start(bf16[2,64,512]{2,1,0:T(8,128)(2,1)} %copy-done.13), channel_id=1, source_target_pairs={{1,8},{2,9},{3,10},{4,11},{5,12},{6,13},{7,14},{9,16},{10,17},{11,... | collective-permute-start | bytes 393224 | tf_op jit(solution)/shard_map/ppermute | solution.py:293
  190.8 118.2 %collective-permute-start.20 = (bf16[32,64,512]{2,1,0:T(8,128)(2,1)}, bf16[32,64,512]{2,1,0:T(8,128)(2,1)}, u32[]{:S(2)}, u32[]{:S(2)}) collective-permute-start(bf16[32,64,512]{2,1,0:T(8,128)(2,1)} %get-tuple-element.103), channel_id=1, source_target_pairs={{8,0},{16,8},{9,1},{17,9},{10,2},{18,10},{11,3},{19,11},{12,4},{20... | collective-permute-start | bytes 6291464 | tf_op jit(solution)/shard_map/ppermute | solution.py:296
  194.0 135.9 %collective-permute-start.17 = (bf16[32,64,512]{2,1,0:T(8,128)(2,1)}, bf16[32,64,512]{2,1,0:T(8,128)(2,1)}, u32[]{:S(2)}, u32[]{:S(2)}) collective-permute-start(bf16[32,64,512]{2,1,0:T(8,128)(2,1)} %get-tuple-element.100), channel_id=1, source_target_pairs={{8,16},{16,24},{9,17},{17,25},{10,18},{18,26},{11,19},{19,27},{12,... | collective-permute-start | bytes 6291464 | tf_op jit(solution)/shard_map/ppermute | solution.py:296
  196.0 2.8 collective-permute-start.21
  196.8 112.1 %collective-permute-start.22 = (bf16[2,64,512]{2,1,0:T(8,128)(2,1)}, bf16[2,64,512]{2,1,0:T(8,128)(2,1)S(1)}, u32[]{:S(2)}, u32[]{:S(2)}) collective-permute-start(bf16[2,64,512]{2,1,0:T(8,128)(2,1)} %copy-done.22), channel_id=1, source_target_pairs={{9,0},{10,1},{11,2},{12,3},{13,4},{14,5},{15,6},{17,8},{18,9},{19,... | collective-permute-start | bytes 393224 | tf_op jit(solution)/shard_map/ppermute | solution.py:293
  198.1 131.8 %collective-permute-start.18 = (bf16[2,64,512]{2,1,0:T(8,128)(2,1)}, bf16[2,64,512]{2,1,0:T(8,128)(2,1)S(1)}, u32[]{:S(2)}, u32[]{:S(2)}) collective-permute-start(bf16[2,64,512]{2,1,0:T(8,128)(2,1)} %copy-done.23), channel_id=1, source_target_pairs={{8,17},{9,18},{10,19},{11,20},{12,21},{13,22},{14,23},{16,25},{17,... | collective-permute-start | bytes 393224 | tf_op jit(solution)/shard_map/ppermute | solution.py:290
  198.8 131.2 %collective-permute-start.19 = (bf16[2,64,512]{2,1,0:T(8,128)(2,1)}, bf16[2,64,512]{2,1,0:T(8,128)(2,1)S(1)}, u32[]{:S(2)}, u32[]{:S(2)}) collective-permute-start(bf16[2,64,512]{2,1,0:T(8,128)(2,1)} %copy-done.21), channel_id=1, source_target_pairs={{9,16},{10,17},{11,18},{12,19},{13,20},{14,21},{15,22},{17,24},{18... | collective-permute-start | bytes 393224 | tf_op jit(solution)/shard_map/ppermute | solution.py:293
  229.0 99.6 %copy-start.9 = (f32[512,512]{1,0:T(8,128)}, f32[512,512]{1,0:T(8,128)S(1)}, u32[]{:S(2)}) copy-start(f32[512,512]{1,0:T(8,128)S(1)} %get-tuple-element.130) | copy-start | bytes 3145732
  328.6 78.7 %collective-permute-start.26 = (bf16[32,64,512]{2,1,0:T(8,128)(2,1)}, bf16[32,64,512]{2,1,0:T(8,128)(2,1)}, u32[]{:S(2)}, u32[]{:S(2)}) collective-permute-start(bf16[32,64,512]{2,1,0:T(8,128)(2,1)} %get-tuple-element.117), channel_id=1, source_target_pairs={{8,0},{9,1},{10,2},{11,3},{12,4},{13,5},{14,6},{15,7}} | collective-permute-start | bytes 6291464 | tf_op jit(solution)/shard_map/ppermute | solution.py:296
  331.9 95.2 %collective-permute-start.23 = (bf16[32,64,512]{2,1,0:T(8,128)(2,1)}, bf16[32,64,512]{2,1,0:T(8,128)(2,1)}, u32[]{:S(2)}, u32[]{:S(2)}) collective-permute-start(bf16[32,64,512]{2,1,0:T(8,128)(2,1)} %get-tuple-element.114), channel_id=1, source_target_pairs={{16,24},{17,25},{18,26},{19,27},{20,28},{21,29},{22,30},{23,31}} | collective-permute-start | bytes 6291464 | tf_op jit(solution)/shard_map/ppermute | solution.py:296
  334.6 8.0 %collective-permute-start.27 = (bf16[2,64,512]{2,1,0:T(8,128)(2,1)}, bf16[2,64,512]{2,1,0:T(8,128)(2,1)S(1)}, u32[]{:S(2)}, u32[]{:S(2)}) collective-permute-start(bf16[2,64,512]{2,1,0:T(8,128)(2,1)} %copy-done.20), channel_id=1, source_target_pairs={{8,1},{9,2},{10,3},{11,4},{12,5},{13,6},{14,7}} | collective-permute-start | bytes 393224 | tf_op jit(solution)/shard_map/ppermute | solution.py:290
  335.3 72.0 %collective-permute-start.28 = (bf16[2,64,512]{2,1,0:T(8,128)(2,1)}, bf16[2,64,512]{2,1,0:T(8,128)(2,1)S(1)}, u32[]{:S(2)}, u32[]{:S(2)}) collective-permute-start(bf16[2,64,512]{2,1,0:T(8,128)(2,1)} %copy-done.16), channel_id=1, source_target_pairs={{9,0},{10,1},{11,2},{12,3},{13,4},{14,5},{15,6}} | collective-permute-start | bytes 393224 | tf_op jit(solution)/shard_map/ppermute | solution.py:293
  341.9 85.2 %collective-permute-start.24 = (bf16[2,64,512]{2,1,0:T(8,128)(2,1)}, bf16[2,64,512]{2,1,0:T(8,128)(2,1)S(1)}, u32[]{:S(2)}, u32[]{:S(2)}) collective-permute-start(bf16[2,64,512]{2,1,0:T(8,128)(2,1)} %copy-done.18), channel_id=1, source_target_pairs={{16,25},{17,26},{18,27},{19,28},{20,29},{21,30},{22,31}} | collective-permute-start | bytes 393224 | tf_op jit(solution)/shard_map/ppermute | solution.py:290
  342.6 84.6 %collective-permute-start.25 = (bf16[2,64,512]{2,1,0:T(8,128)(2,1)}, bf16[2,64,512]{2,1,0:T(8,128)(2,1)S(1)}, u32[]{:S(2)}, u32[]{:S(2)}) collective-permute-start(bf16[2,64,512]{2,1,0:T(8,128)(2,1)} %copy-done.17), channel_id=1, source_target_pairs={{17,24},{18,25},{19,26},{20,27},{21,28},{22,29},{23,30}} | collective-permute-start | bytes 393224 | tf_op jit(solution)/shard_map/ppermute | solution.py:293
  552.0 5.6 collective-permute-start.29
  (30 other events, 165.7 us)
Sparse Core Ops, SparseCore 0:
  455.9 95.1 reduce-scatter.1

commit v2 on v1

--- a/solution.py
+++ b/solution.py
@@ -12,7 +12,7 @@
 LANES = 128
 CT = jnp.bfloat16
 TILE = 16
-ANY = pl.BlockSpec(memory_space=pl.ANY)
+ANY = pl.BlockSpec(memory_space=pltpu.HBM)
 SMEM = pl.BlockSpec(memory_space=pltpu.SMEM)
 
 
@@ -54,8 +54,8 @@
 def chain_kernel(replica, rows, cols, fresh, *refs):
     meta, recv, recv_top, recv_bot, entry, entry_top, entry_bot, masks, mask_top, mask_bot, weight, kern = refs[:12]
     refs = refs[12 if fresh else 15 :]
-    sent, sent_top, sent_bot, outs, mixed, gates = refs[:6]
-    up, seen, seen_halo, wbuf, kbuf, taps, bm, out, sems = refs[6:]
+    sent, outs, mixed, gates = refs[:4]
+    up, seen, seen_halo, wbuf, kbuf, taps, bm, out, sems = refs[4:]
     channels = up.shape[2]
     micro = meta[1]
 
@@ -130,8 +130,6 @@
 
         stores = [
             pltpu.make_async_copy(out, sent, sems.at[2]),
-            pltpu.make_async_copy(out.at[pl.ds(0, 2)], sent_top, sems.at[3]),
-            pltpu.make_async_copy(out.at[pl.ds(rows - 2, 2)], sent_bot, sems.at[4]),
             pltpu.make_async_copy(out, outs.at[replica, micro], sems.at[5]),
         ]
         for store in stores:
@@ -147,16 +145,15 @@
     micro = masks[0].shape[3]
     fresh = buffers is None
     strip = jax.ShapeDtypeStruct((rows, cols, channels), jnp.bfloat16)
-    edge = jax.ShapeDtypeStruct((2, cols, channels), jnp.bfloat16)
     whole = jax.ShapeDtypeStruct((2, micro, rows, cols, channels), jnp.bfloat16)
     operands = [meta, *recv, *entry, *masks, weight, kern]
     if not fresh:
         operands += list(buffers)
     results = pl.pallas_call(
         functools.partial(chain_kernel, replica, rows, cols, fresh),
-        out_shape=(strip, edge, edge, whole, whole, whole),
+        out_shape=(strip, whole, whole, whole),
         in_specs=[SMEM] + [ANY] * (len(operands) - 1),
-        out_specs=(ANY,) * 6,
+        out_specs=(ANY,) * 4,
         scratch_shapes=[
             pltpu.VMEM((rows + 4, cols, channels), jnp.bfloat16),
             pltpu.VMEM((rows, cols, channels), jnp.int32),
@@ -168,14 +165,71 @@
             pltpu.VMEM((rows, cols, channels), jnp.bfloat16),
             pltpu.SemaphoreType.DMA((8,)),
         ],
-        input_output_aliases={} if fresh else {12: 3, 13: 4, 14: 5},
-        compiler_params=pltpu.CompilerParams(vmem_limit_bytes=40 << 20),
+        input_output_aliases={} if fresh else {12: 1, 13: 2, 14: 3},
+        compiler_params=pltpu.CompilerParams(vmem_limit_bytes=60 << 20),
         cost_estimate=pl.CostEstimate(flops=60 * rows * cols * channels * 10, bytes_accessed=16 << 20, transcendentals=0),
     )(*operands)
-    return results[:3], results[3:]
-
-
-def grads_kernel(rows, cols, meta, acts, act_top, act_bot, kern, _mixed, _gates, wgrad, kgrad, mixed, gates, framed, kbuf, taps, bm, gated, depth, wsum, ksum, kout, sems):
+    return results[0], results[1:]
+
+
+def depth_kernel_body(rows, cols, meta, acts, act_top, act_bot, kern, _mixed, result, mixed, framed, kbuf, taps, depth, sems):
+    channels = framed.shape[2]
+    replica = meta[0]
+    micro = meta[1]
+    loads = [
+        pltpu.make_async_copy(acts.at[replica, 0, 0, micro, 0], framed.at[pl.ds(2, rows)], sems.at[0]),
+        pltpu.make_async_copy(act_top.at[replica, micro], framed.at[pl.ds(0, 2)], sems.at[1]),
+        pltpu.make_async_copy(act_bot.at[replica, micro], framed.at[pl.ds(rows + 2, 2)], sems.at[2]),
+        pltpu.make_async_copy(kern.at[replica], kbuf, sems.at[3]),
+    ]
+    for load in loads:
+        load.start()
+    for load in loads:
+        load.wait()
+    spread_kernel(kbuf, taps)
+    column = lax.broadcasted_iota(jnp.int32, (cols, LANES), 0)
+
+    @pl.loop(0, channels // LANES)
+    def _(block):
+        lanes = lane_block(block)
+
+        @pl.loop(0, rows)
+        def _(row):
+            depth[row, :, lanes] = row_conv(framed, row, lanes, taps, cols, column, 1).astype(jnp.bfloat16)
+
+    store = pltpu.make_async_copy(depth, result, sems.at[0])
+    store.start()
+    store.wait()
+
+
+def depth_step(meta, acts, kern, mixed):
+    _, _, _, micro, _, rows, cols, channels = acts[0].shape
+    return pl.pallas_call(
+        functools.partial(depth_kernel_body, rows, cols),
+        out_shape=(
+            jax.ShapeDtypeStruct((rows, cols, channels), jnp.bfloat16),
+            jax.ShapeDtypeStruct(mixed.shape, mixed.dtype),
+        ),
+        in_specs=[SMEM] + [ANY] * 5,
+        out_specs=(ANY,) * 2,
+        scratch_shapes=[
+            pltpu.VMEM((rows + 4, cols, channels), jnp.bfloat16),
+            pltpu.VMEM((25, channels), jnp.float32),
+            pltpu.VMEM((25, TILE, channels), CT),
+            pltpu.VMEM((rows, cols, channels), jnp.bfloat16),
+            pltpu.SemaphoreType.DMA((4,)),
+        ],
+        input_output_aliases={5: 1},
+        compiler_params=pltpu.CompilerParams(vmem_limit_bytes=60 << 20),
+        cost_estimate=pl.CostEstimate(flops=60 * rows * cols * channels * 10, bytes_accessed=4 << 20, transcendentals=0),
+    )(meta, *acts, kern, mixed)
+
+
+def grads_kernel(rows, cols, given, *refs):
+    meta, acts, act_top, act_bot, kern = refs[:5]
+    ready_depth = refs[7] if given else None
+    refs = refs[8 if given else 7 :]
+    wgrad, kgrad, mixed, gates, framed, kbuf, taps, bm, gated, depth, wsum, ksum, kout, sems = refs
     channels = framed.shape[2]
     replica = meta[0]
     micro = meta[1]
@@ -187,6 +241,8 @@
         pltpu.make_async_copy(mixed.at[replica, micro], bm, sems.at[4]),
         pltpu.make_async_copy(gates.at[replica, micro], gated, sems.at[5]),
     ]
+    if given:
+        loads.append(pltpu.make_async_copy(ready_depth, depth, sems.at[6]))
     for load in loads:
         load.start()
     for load in loads:
@@ -199,9 +255,10 @@
     def _(block):
         lanes = lane_block(block)
 
-        @pl.loop(0, rows)
-        def _(row):
-            depth[row, :, lanes] = row_conv(framed, row, lanes, taps, cols, column, 1).astype(jnp.bfloat16)
+        if not given:
+            @pl.loop(0, rows)
+            def _(row):
+                depth[row, :, lanes] = row_conv(framed, row, lanes, taps, cols, column, 1).astype(jnp.bfloat16)
 
         @pl.loop(0, rows)
         def _(row):
@@ -241,19 +298,19 @@
         store.wait()
 
 
-def grads_step(meta, acts, kern, mixed, gates):
+def grads_step(meta, acts, kern, mixed, gates, depth):
     _, _, _, micro, _, rows, cols, channels = acts[0].shape
     strip = pltpu.VMEM((rows, cols, channels), jnp.bfloat16)
     whole = jax.ShapeDtypeStruct((2, micro, rows, cols, channels), jnp.bfloat16)
     return pl.pallas_call(
-        functools.partial(grads_kernel, rows, cols),
+        functools.partial(grads_kernel, rows, cols, depth is not None),
         out_shape=(
             jax.ShapeDtypeStruct((channels, channels), jnp.float32),
             jax.ShapeDtypeStruct((25, channels), jnp.float32),
             whole,
             whole,
         ),
-        in_specs=[SMEM] + [ANY] * 6,
+        in_specs=[SMEM] + [ANY] * (6 if depth is None else 7),
         out_specs=(ANY,) * 4,
         scratch_shapes=[
             pltpu.VMEM((rows + 4, cols, channels), jnp.bfloat16),
@@ -265,12 +322,12 @@
             pltpu.VMEM((channels, channels), jnp.float32),
             pltpu.VMEM((25, 8, channels), jnp.float32),
             pltpu.VMEM((25, channels), jnp.float32),
-            pltpu.SemaphoreType.DMA((6,)),
+            pltpu.SemaphoreType.DMA((7,)),
         ],
         input_output_aliases={5: 2, 6: 3},
-        compiler_params=pltpu.CompilerParams(vmem_limit_bytes=40 << 20),
+        compiler_params=pltpu.CompilerParams(vmem_limit_bytes=60 << 20),
         cost_estimate=pl.CostEstimate(flops=120 * rows * cols * channels * 10, bytes_accessed=8 << 20, transcendentals=0),
-    )(meta, *acts, kern, mixed, gates)
+    )(meta, *acts, kern, mixed, gates, *([] if depth is None else [depth]))
 
 
 def edges(cells, dim):
@@ -283,18 +340,28 @@
     return above, below
 
 
-def passed_along(values, by, sources):
-    main, head, tail = values
+def passed_along(main, by, sources):
+    return lax.ppermute(main, "sec", [(p, p + by) for p in sources])
+
+
+def strip_sums(wide, taps):
     count = lax.axis_size("strip")
-    axes = ("sec", "strip")
-    above = lax.ppermute(
-        tail, axes, [(p * count + z, (p + by) * count + z + 1) for p in sources for z in range(count - 1)]
-    )
-    below = lax.ppermute(
-        head, axes, [(p * count + z + 1, (p + by) * count + z) for p in sources for z in range(count - 1)]
-    )
-    main = lax.ppermute(main, "sec", [(p, p + by) for p in sources])
-    return main, above, below
+    place = lax.axis_index("strip")
+    steps = count.bit_length() - 1
+    share = wide.shape[0] // count
+    columns = wide.shape[1]
+    blocks = wide.reshape(count, share, columns)
+    for step in range(steps):
+        side = (place >> step) & 1
+        pairs = blocks.reshape(-1, 2, share, columns)
+        kept = lax.dynamic_index_in_dim(pairs, side, 1, keepdims=False)
+        given = lax.dynamic_index_in_dim(pairs, 1 - side, 1, keepdims=False)
+        sent = jnp.concatenate([given.reshape(-1, columns), taps]).astype(jnp.bfloat16)
+        got = lax.ppermute(sent, "strip", [(i, i ^ (1 << step)) for i in range(count)]).astype(jnp.float32)
+        rows = got.shape[0] - taps.shape[0]
+        blocks = kept + got[:rows].reshape(kept.shape)
+        taps = taps + got[rows:]
+    return blocks.reshape(share, columns), taps
 
 
 def timetable(sections, micro):
@@ -359,27 +426,37 @@
                     and 0 <= tick - (sections - 1 - p if replica == 0 else p) < micro
                 ]
                 received[replica] = passed_along(values, by, sources)
+        if tick == 0:
+            outs, mixed, gates = buffers
+            early, mixed = depth_step(table[2 * micro - 1], acts, kernels, mixed)
+            latest = early
+            buffers = (outs, mixed, gates)
         for k in range(2 * micro):
             if ready[k] != tick:
                 continue
             run = table[k]
             outs, mixed, gates = buffers
-            wgrad, kgrad, mixed, gates = grads_step(run, acts, kernels, mixed, gates)
+            given = early if k == 2 * micro - 1 else None
+            wgrad, kgrad, mixed, gates = grads_step(run, acts, kernels, mixed, gates, given)
+            latest = kgrad
             buffers = (outs, mixed, gates)
             for replica in range(2):
                 mine = run[0] == replica
                 grads_w[replica] = grads_w[replica] + jnp.where(mine, wgrad, 0.0)
                 grads_k[replica] = grads_k[replica] + jnp.where(mine, kgrad, 0.0)
 
+        if tick < ticks - 1:
+            for replica in range(2):
+                main, _ = lax.optimization_barrier((received[replica], latest))
+                received[replica] = (main, *edges(main, 0))
+
     factor = 1.0 / H
-    both_w = jnp.concatenate(grads_w, axis=1).astype(jnp.bfloat16)
-    shares = lax.psum_scatter(both_w, "strip", scatter_dimension=0, tiled=True).astype(jnp.float32)
-    kernel_all = lax.psum(jnp.stack(grads_k).astype(jnp.bfloat16), "strip").astype(jnp.float32)
+    shares, kernel_all = strip_sums(jnp.concatenate(grads_w, axis=1), jnp.concatenate(grads_k, axis=1))
     share_rows = shares.shape[0]
-    partner = jnp.concatenate([shares[:, channels:], kernel_all[1]], axis=0).astype(jnp.bfloat16)
+    partner = jnp.concatenate([shares[:, channels:], kernel_all[:, channels:]], axis=0).astype(jnp.bfloat16)
     partner = lax.ppermute(partner, "sec", mirror).astype(jnp.float32)
     share_w = (shares[:, :channels] + partner[:share_rows]) * factor
-    full_k = (kernel_all[0] + partner[share_rows:]) * factor
+    full_k = (kernel_all[:, :channels] + partner[share_rows:]) * factor
     return buffers[0][:, None, :, None], share_w[None, None], full_k[None, None]
 
 

time: 568 us -> 471 us (0.83)
  blocking collectives: 90.4 us -> 0 us
  starting transfers between devices: 59.3 us -> 114 us
  waiting for transfers between devices: 171 us -> 120 us
  local copies, waits for them, and re-layouts: 42.6 us -> 25.1 us
  between operations: 20.1 us -> 6.94 us
  Pallas kernels: 174 us -> 186 us
  other arithmetic: 8.95 us -> 17.4 us
    psum x1 -> x0, blocking collectives: 90.4 us -> none  [body(): lax.psum(jnp.stack(grads_k).astype(jnp.bfloat16), 'strip')]
    ppermute x2 -> x10, starting transfers between devices: 3.62 us -> 61.7 us  [edges(): above = lax.ppermute(tail, 'strip', [(i, i + 1) for i in range(count - 1)])]
    ppermute x24 -> x11, waiting for transfers between devices: 148 us -> 96.6 us  [the longest x8 78.1 us: passed_along(): return lax.ppermute(main, 'sec', [(p, p + by) for p in sources])]
    ppermute x24 -> x11, starting transfers between devices: 47.2 us -> 22.2 us  [the longest x8 14.6 us: passed_along(): return lax.ppermute(main, 'sec', [(p, p + by) for p in sources])]
    unnamed x63, local copies, waits for them, and re-layouts: 31.7 us -> 8.08 us
    ppermute x1, starting transfers between devices: 2.01 us -> 13.2 us  [body(): partner = lax.ppermute(partner, 'sec', mirror).astype(jnp.float32)]
    pallas_call x4 -> x5, Pallas kernels: 91.2 us -> 102 us  [the longest x4 87.6 us: grads_step(): pl.pallas_call(functools.partial(grads_kernel, rows, cols, depth is not N...]
    ppermute x2 -> x10, starting transfers between devices: 2.57 us -> 12.9 us  [edges(): below = lax.ppermute(head, 'strip', [(i + 1, i) for i in range(count - 1)])]
  transfers between devices with their start and end apart: 31 -> 33, of which waited for: 7 -> 14; matrix products, arithmetic and copies ran while one was open for 2% -> 5% of each run, Pallas kernels for 26% -> 32%
where the time goes in v2:
time: 471 us; the launch traced here: 470 us
  Pallas kernels  186 us (39%)
  waiting for transfers between devices  120 us (25%)
  starting transfers between devices  114 us (24%)
  local copies, waits for them, and re-layouts  25.1 us (5%)
  other arithmetic  17.4 us (4%)
  between operations  6.94 us (1%)
    pallas_call x4, Pallas kernels, grads_step(): pl.pallas_call(functools.partial(grads_kernel, rows, cols, depth is not N...  87.6 us
    pallas_call x10, Pallas kernels, chain_step(): pl.pallas_call(functools.partial(chain_kernel, replica, rows, cols, fresh...  84.5 us
    ppermute x8, waiting for transfers between devices, passed_along(): return lax.ppermute(main, 'sec', [(p, p + by) for p in sources])  78.1 us
    ppermute x10, starting transfers between devices, edges(): above = lax.ppermute(tail, 'strip', [(i, i + 1) for i in range(count - 1)])  61.7 us
    ppermute x3, waiting for transfers between devices, strip_sums(): lax.ppermute(sent, 'strip', [(i, i ^ 1 << step) for i in range(count)])  18.5 us
    ppermute x10, waiting for transfers between devices, edges(): below = lax.ppermute(head, 'strip', [(i + 1, i) for i in range(count - 1)])  18.1 us
    ppermute x8, starting transfers between devices, passed_along(): return lax.ppermute(main, 'sec', [(p, p + by) for p in sources])  14.6 us
    pallas_call x1, Pallas kernels, depth_step(): pl.pallas_call(functools.partial(depth_kernel_body, rows, cols), out_shap...  14 us
  transfers between devices with their start and end apart: 33, of which 14 were waited for; matrix products, arithmetic and copies ran while one was open for 5% of the time, Pallas kernels for 32%

profile of v2, /device:TPU:0, one launch (start us, length us, event | category | flops | bytes accessed | tf_op | source)
XLA Modules:
  0.0 469.9 jit_solution(5665113562952620963)
XLA Ops:
  2.6 3.9 collective-permute-start.2
  12.7 3.1 collective-permute-start
  16.5 2.8 collective-permute-done.2
  28.3 20.0 %shard_map.86 = (bf16[32,64,512]{2,1,0:T(8,128)(2,1)}, bf16[2,2,32,64,512]{4,3,2,1,0:T(8,128)(2,1)}, bf16[2,2,32,64,512]{4,3,2,1,0:T(8,128)(2,1)}, bf16[2,2,32,64,512]{4,3,2,1,0:T(8,128)(2,1)}) custom-call(s32[3]{0:T(128)} %get-tuple-element.173.refs_0_, ...), custom_call_target="tpu_custom_call", output_to_operand_aliasing={{1}: (12, {}), {2}: (13, {}), {3}: (14, {})} | custom-call | flops 629145600 | bytes 16777216 | tf_op jit(solution)/shard_map/pallas_call | solution.py:152
  51.9 8.7 %collective-permute-start.4 = (bf16[2,2,2,64,512]{4,3,2,1,0:T(8,128)(2,1)}, bf16[2,2,2,64,512]{4,3,2,1,0:T(8,128)(2,1)S(1)}, u32[]{:S(2)}, u32[]{:S(2)}) collective-permute-start(bf16[2,2,2,64,512]{4,3,2,1,0:T(8,128)(2,1)} %get-tuple-element.136), channel_id=1, source_target_pairs={{0,1},{1,2},{2,3},{3,4},{4,5},{5,6},{6,7},{8,9},{9,10},{10,11},{11... | collective-permute-start | bytes 1572872 | tf_op jit(solution)/shard_map/ppermute | solution.py:338
  63.2 3.3 collective-permute-done.5.act_bot.refs_3_
  67.3 14.0 %shard_map.87 = (bf16[32,64,512]{2,1,0:T(8,128)(2,1)}, bf16[2,2,32,64,512]{4,3,2,1,0:T(8,128)(2,1)}) custom-call(s32[2]{0:T(128)} %get-tuple-element.172.meta.refs_0_, bf16[2,1,1,2,1,32,64,512]{7,6,5,4,3,2,1,0:T(8,128)(2,1)} %refs_1_.7, bf16[2,2,2,64,512]{4,3,2,1,0:T(8,128)(2,1)} %copy-done, ...), custom_call_target="tpu_custom_call", output_to_operand_aliasing={{1}: (5, {})} | custom-call | flops 629145600 | bytes 4194304 | tf_op jit(solution)/shard_map/pallas_call | solution.py:207
  83.6 9.7 %collective-permute-start.9 = (bf16[2,64,512]{2,1,0:T(8,128)(2,1)S(1)}, bf16[2,64,512]{2,1,0:T(8,128)(2,1)S(1)}, u32[]{:S(2)}, u32[]{:S(2)}) collective-permute-start(bf16[2,64,512]{2,1,0:T(8,128)(2,1)S(1)} %get-tuple-element.154), channel_id=1, source_target_pairs={{0,1},{1,2},{2,3},{3,4},{4,5},{5,6},{6,7},{8,9},{9,10},{10,11},{11... | collective-permute-start | bytes 393224 | tf_op jit(solution)/shard_map/ppermute | solution.py:338
  98.1 4.3 collective-permute-start.6
  104.4 7.6 %collective-permute-done.7.refs_3_ = bf16[2,64,512]{2,1,0:T(8,128)(2,1)S(1)} collective-permute-done((bf16[2,64,512]{2,1,0:T(8,128)(2,1)S(1)}, bf16[2,64,512]{2,1,0:T(8,128)(2,1)S(1)}, u32[]{:S(2)}, u32[]{:S(2)}) %collective-permute-start.7) | collective-permute-done | bytes 131104 | tf_op jit(solution)/shard_map/ppermute | solution.py:339
  112.6 20.0 %shard_map.89 = (bf16[32,64,512]{2,1,0:T(8,128)(2,1)}, bf16[2,2,32,64,512]{4,3,2,1,0:T(8,128)(2,1)}, bf16[2,2,32,64,512]{4,3,2,1,0:T(8,128)(2,1)}, bf16[2,2,32,64,512]{4,3,2,1,0:T(8,128)(2,1)}) custom-call(s32[3]{0:T(128)} %add_add_fusion.3.refs_0_, bf16[32,64,512]{2,1,0:T(8,128)(2,1)} %copy-done.3, ...), custom_call_target="tpu_custom_call", output_to_operand_aliasing={{1}: (12, {}), {2}: (13, {}), {3}: (14, {})} | custom-call | flops 629145600 | bytes 16777216 | tf_op jit(solution)/shard_map/pallas_call | solution.py:152
  132.5 3.7 collective-permute-start.11
  136.3 24.3 %shard_map.90 = (f32[512,512]{1,0:T(8,128)}, f32[25,512]{1,0:T(8,128)}, bf16[2,2,32,64,512]{4,3,2,1,0:T(8,128)(2,1)}, bf16[2,2,32,64,512]{4,3,2,1,0:T(8,128)(2,1)}) custom-call(s32[2]{0:T(128)} %get-tuple-element.171.refs_0_, bf16[2,1,1,2,1,32,64,512]{7,6,5,4,3,2,1,0:T(8,128)(2,1)} %refs_1_.7, ...), custom_call_target="tpu_custom_call", output_to_operand_aliasing={{2}: (5, {}), {3}: (6, {})} | custom-call | flops 1258291200 | bytes 8388608 | tf_op jit(solution)/shard_map/pallas_call | solution.py:305
  161.6 5.2 %collective-permute-start.15 = (bf16[2,64,512]{2,1,0:T(8,128)(2,1)S(1)}, bf16[2,64,512]{2,1,0:T(8,128)(2,1)S(1)}, u32[]{:S(2)}, u32[]{:S(2)}) collective-permute-start(bf16[2,64,512]{2,1,0:T(8,128)(2,1)S(1)} %get-tuple-element.150), channel_id=1, source_target_pairs={{0,1},{1,2},{2,3},{3,4},{4,5},{5,6},{6,7},{8,9},{9,10},{10,11},{11... | collective-permute-start | bytes 393224 | tf_op jit(solution)/shard_map/ppermute | solution.py:338
  168.7 11.1 %collective-permute-done.11.refs_1_ = bf16[32,64,512]{2,1,0:T(8,128)(2,1)S(1)} collective-permute-done((bf16[32,64,512]{2,1,0:T(8,128)(2,1)}, bf16[32,64,512]{2,1,0:T(8,128)(2,1)S(1)}, u32[]{:S(2)}, u32[]{:S(2)}) %collective-permute-start.11) | collective-permute-done | bytes 2097184 | tf_op jit(solution)/shard_map/ppermute | solution.py:344
  182.6 4.7 collective-permute-start.12
  189.3 3.2 collective-permute-done.13.refs_3_
  194.8 24.3 %shard_map.93 = (f32[512,512]{1,0:T(8,128)}, f32[25,512]{1,0:T(8,128)}, bf16[2,2,32,64,512]{4,3,2,1,0:T(8,128)(2,1)}, bf16[2,2,32,64,512]{4,3,2,1,0:T(8,128)(2,1)}) custom-call(s32[2]{0:T(128)} %get-tuple-element.170.refs_0_, bf16[2,1,1,2,1,32,64,512]{7,6,5,4,3,2,1,0:T(8,128)(2,1)} %refs_1_.7, ...), custom_call_target="tpu_custom_call", output_to_operand_aliasing={{2}: (5, {}), {3}: (6, {})} | custom-call | flops 1258291200 | bytes 8388608 | tf_op jit(solution)/shard_map/pallas_call | solution.py:305
  219.0 34.7 %collective-permute-done.20.refs_1_ = bf16[32,64,512]{2,1,0:T(8,128)(2,1)} collective-permute-done((bf16[32,64,512]{2,1,0:T(8,128)(2,1)}, bf16[32,64,512]{2,1,0:T(8,128)(2,1)}, u32[]{:S(2)}, u32[]{:S(2)}) %collective-permute-start.20) | collective-permute-done | bytes 2097184 | tf_op jit(solution)/shard_map/ppermute | solution.py:344
  254.7 7.0 %collective-permute-start.21 = (bf16[2,64,512]{2,1,0:T(8,128)(2,1)S(1)}, bf16[2,64,512]{2,1,0:T(8,128)(2,1)S(1)}, u32[]{:S(2)}, u32[]{:S(2)}) collective-permute-start(bf16[2,64,512]{2,1,0:T(8,128)(2,1)S(1)} %get-tuple-element.146), channel_id=1, source_target_pairs={{0,1},{1,2},{2,3},{3,4},{4,5},{5,6},{6,7},{8,9},{9,10},{10,11},{11... | collective-permute-start | bytes 393224 | tf_op jit(solution)/shard_map/ppermute | solution.py:338
  267.2 20.0 %shard_map.94 = (bf16[32,64,512]{2,1,0:T(8,128)(2,1)}, bf16[2,2,32,64,512]{4,3,2,1,0:T(8,128)(2,1)}, bf16[2,2,32,64,512]{4,3,2,1,0:T(8,128)(2,1)}, bf16[2,2,32,64,512]{4,3,2,1,0:T(8,128)(2,1)}) custom-call(s32[3]{0:T(128)} %add_add_fusion.8.refs_0_, ...), custom_call_target="tpu_custom_call", output_to_operand_aliasing={{1}: (12, {}), {2}: (13, {}), {3}: (14, {})} | custom-call | flops 629145600 | bytes 16777216 | tf_op jit(solution)/shard_map/pallas_call | solution.py:152
  289.5 5.5 %collective-permute-start.18 = (bf16[2,64,512]{2,1,0:T(8,128)(2,1)S(1)}, bf16[2,64,512]{2,1,0:T(8,128)(2,1)S(1)}, u32[]{:S(2)}, u32[]{:S(2)}) collective-permute-start(bf16[2,64,512]{2,1,0:T(8,128)(2,1)S(1)} %get-tuple-element.148), channel_id=1, source_target_pairs={{0,1},{1,2},{2,3},{3,4},{4,5},{5,6},{6,7},{8,9},{9,10},{10,11},{11... | collective-permute-start | bytes 393224 | tf_op jit(solution)/shard_map/ppermute | solution.py:338
  308.2 24.3 %shard_map.96 = (f32[512,512]{1,0:T(8,128)}, f32[25,512]{1,0:T(8,128)}, bf16[2,2,32,64,512]{4,3,2,1,0:T(8,128)(2,1)}, bf16[2,2,32,64,512]{4,3,2,1,0:T(8,128)(2,1)}) custom-call(s32[2]{0:T(128)} %get-tuple-element.169.refs_0_, bf16[2,1,1,2,1,32,64,512]{7,6,5,4,3,2,1,0:T(8,128)(2,1)} %refs_1_.7, ...), custom_call_target="tpu_custom_call", output_to_operand_aliasing={{2}: (5, {}), {3}: (6, {})} | custom-call | flops 1258291200 | bytes 8388608 | tf_op jit(solution)/shard_map/pallas_call | solution.py:305
  332.5 32.3 %collective-permute-done.26.refs_1_ = bf16[32,64,512]{2,1,0:T(8,128)(2,1)S(1)} collective-permute-done((bf16[32,64,512]{2,1,0:T(8,128)(2,1)}, bf16[32,64,512]{2,1,0:T(8,128)(2,1)S(1)}, u32[]{:S(2)}, u32[]{:S(2)}) %collective-permute-start.26) | collective-permute-done | bytes 2097184 | tf_op jit(solution)/shard_map/ppermute | solution.py:344
  364.8 3.9 collective-permute-start.27
  371.0 9.8 %collective-permute-start.24 = (bf16[2,64,512]{2,1,0:T(8,128)(2,1)S(1)}, bf16[2,64,512]{2,1,0:T(8,128)(2,1)S(1)}, u32[]{:S(2)}, u32[]{:S(2)}) collective-permute-start(bf16[2,64,512]{2,1,0:T(8,128)(2,1)S(1)} %get-tuple-element.144), channel_id=1, source_target_pairs={{0,1},{1,2},{2,3},{3,4},{4,5},{5,6},{6,7},{8,9},{9,10},{10,11},{11... | collective-permute-start | bytes 393224 | tf_op jit(solution)/shard_map/ppermute | solution.py:338
  383.4 20.0 %shard_map.97 = (bf16[32,64,512]{2,1,0:T(8,128)(2,1)}, bf16[2,2,32,64,512]{4,3,2,1,0:T(8,128)(2,1)}, bf16[2,2,32,64,512]{4,3,2,1,0:T(8,128)(2,1)}, bf16[2,2,32,64,512]{4,3,2,1,0:T(8,128)(2,1)}) custom-call(s32[3]{0:T(128)} %add_add_fusion.9.refs_0_, bf16[32,64,512]{2,1,0:T(8,128)(2,1)} %copy-done.2, ...), custom_call_target="tpu_custom_call", output_to_operand_aliasing={{1}: (12, {}), {2}: (13, {}), {3}: (14, {})} | custom-call | flops 629145600 | bytes 16777216 | tf_op jit(solution)/shard_map/pallas_call | solution.py:152
  405.0 14.8 %shard_map.99 = (f32[512,512]{1,0:T(8,128)}, f32[25,512]{1,0:T(8,128)}, bf16[2,2,32,64,512]{4,3,2,1,0:T(8,128)(2,1)}, bf16[2,2,32,64,512]{4,3,2,1,0:T(8,128)(2,1)}) custom-call(s32[2]{0:T(128)} %get-tuple-element.172.meta.refs_0_, bf16[2,1,1,2,1,32,64,512]{7,6,5,4,3,2,1,0:T(8,128)(2,1)} %refs_1_.7, ...), custom_call_target="tpu_custom_call", output_to_operand_aliasing={{2}: (5, {}), {3}: (6, {})} | custom-call | flops 1258291200 | bytes 8388608 | tf_op jit(solution)/shard_map/pallas_call | solution.py:305
  430.4 8.2 %collective-permute-done.30 = bf16[153,1024]{1,0:T(8,128)(2,1)S(1)} collective-permute-done((bf16[153,1024]{1,0:T(8,128)(2,1)S(1)}, bf16[153,1024]{1,0:T(8,128)(2,1)S(1)}, u32[]{:S(2)}, u32[]{:S(2)}) %collective-permute-start.30) | collective-permute-done | bytes 313376 | tf_op jit(solution)/shard_map/ppermute | solution.py:360
  439.9 3.0 collective-permute-start.31
  442.9 8.8 %collective-permute-done.31 = bf16[89,1024]{1,0:T(8,128)(2,1)S(1)} collective-permute-done((bf16[89,1024]{1,0:T(8,128)(2,1)S(1)}, bf16[89,1024]{1,0:T(8,128)(2,1)S(1)}, u32[]{:S(2)}, u32[]{:S(2)}) %collective-permute-start.31) | collective-permute-done | bytes 182304 | tf_op jit(solution)/shard_map/ppermute | solution.py:360
  452.7 13.2 %collective-permute-start.32 = (bf16[89,512]{1,0:T(8,128)(2,1)S(1)}, bf16[89,512]{1,0:T(8,128)(2,1)S(1)}, u32[]{:S(2)}, u32[]{:S(2)}) collective-permute-start(bf16[89,512]{1,0:T(8,128)(2,1)S(1)} %pad_maximum_fusion.8), channel_id=1, source_target_pairs={{0,24},{8,16},{16,8},{24,0},{1,25},{9,17},{17,9},{25,1},{2,26},{10... | collective-permute-start | bytes 273416 | tf_op jit(solution)/shard_map/ppermute | solution.py:457
  (175 shorter events, 83.9 us)
Async XLA Ops:
  2.6 16.7 %collective-permute-start.2 = (bf16[537,512]{1,0:T(8,128)(2,1)}, bf16[537,512]{1,0:T(8,128)(2,1)S(1)}, u32[]{:S(2)}, u32[]{:S(2)}) collective-permute-start(bf16[537,512]{1,0:T(8,128)(2,1)} %pad_maximum_fusion.4), channel_id=1, source_target_pairs={{0,24},{8,16},{16,8},{24,0},{1,25},{9,17},{17,9},{25,1},{2,26},{10... | collective-permute-start | bytes 1649672 | tf_op jit(solution)/shard_map/ppermute | solution.py:391
  11.4 9.7 %collective-permute-start.1 = (bf16[2,2,2,2,64,512]{5,4,3,2,1,0:T(8,128)(2,1)}, bf16[2,2,2,2,64,512]{5,4,3,2,1,0:T(8,128)(2,1)S(1)}, u32[]{:S(2)}, u32[]{:S(2)}) collective-permute-start(bf16[2,2,2,2,64,512]{5,4,3,2,1,0:T(8,128)(2,1)} %get-tuple-element.157), channel_id=1, source_target_pairs={{1,0},{2,1},{3,2},{4,3},{5,4},{6,5},{7,6},{9,8},{10,9},{11,10},{12... | collective-permute-start | bytes 3145736 | tf_op jit(solution)/shard_map/ppermute | solution.py:339
  12.7 9.5 %collective-permute-start = (bf16[2,2,2,2,64,512]{5,4,3,2,1,0:T(8,128)(2,1)}, bf16[2,2,2,2,64,512]{5,4,3,2,1,0:T(8,128)(2,1)S(1)}, u32[]{:S(2)}, u32[]{:S(2)}) collective-permute-start(bf16[2,2,2,2,64,512]{5,4,3,2,1,0:T(8,128)(2,1)} %get-tuple-element.158), channel_id=1, source_target_pairs={{0,1},{1,2},{2,3},{3,4},{4,5},{5,6},{6,7},{8,9},{9,10},{10,11},{11... | collective-permute-start | bytes 3145736 | tf_op jit(solution)/shard_map/ppermute | solution.py:338
  26.3 55.1 %collective-permute-start.8 = (bf16[32,64,512]{2,1,0:T(8,128)(2,1)}, bf16[32,64,512]{2,1,0:T(8,128)(2,1)}, u32[]{:S(2)}, u32[]{:S(2)}) collective-permute-start(bf16[32,64,512]{2,1,0:T(8,128)(2,1)} %get-tuple-element.72), channel_id=1, source_target_pairs={{24,16},{25,17},{26,18},{27,19},{28,20},{29,21},{30,22},{31,23}} | collective-permute-start | bytes 6291464 | tf_op jit(solution)/shard_map/ppermute | solution.py:344
  48.2 45.8 %collective-permute-start.3 = (bf16[32,64,512]{2,1,0:T(8,128)(2,1)}, bf16[32,64,512]{2,1,0:T(8,128)(2,1)S(1)}, u32[]{:S(2)}, u32[]{:S(2)}) collective-permute-start(bf16[32,64,512]{2,1,0:T(8,128)(2,1)} %get-tuple-element.68), channel_id=1, source_target_pairs={{0,8},{1,9},{2,10},{3,11},{4,12},{5,13},{6,14},{7,15}} | collective-permute-start | bytes 6291464 | tf_op jit(solution)/shard_map/ppermute | solution.py:344
  51.9 11.3 %collective-permute-start.4 = (bf16[2,2,2,64,512]{4,3,2,1,0:T(8,128)(2,1)}, bf16[2,2,2,64,512]{4,3,2,1,0:T(8,128)(2,1)S(1)}, u32[]{:S(2)}, u32[]{:S(2)}) collective-permute-start(bf16[2,2,2,64,512]{4,3,2,1,0:T(8,128)(2,1)} %get-tuple-element.136), channel_id=1, source_target_pairs={{0,1},{1,2},{2,3},{3,4},{4,5},{5,6},{6,7},{8,9},{9,10},{10,11},{11... | collective-permute-start | bytes 1572872 | tf_op jit(solution)/shard_map/ppermute | solution.py:338
  60.6 5.9 %collective-permute-start.5 = (bf16[2,2,2,64,512]{4,3,2,1,0:T(8,128)(2,1)}, bf16[2,2,2,64,512]{4,3,2,1,0:T(8,128)(2,1)S(1)}, u32[]{:S(2)}, u32[]{:S(2)}) collective-permute-start(bf16[2,2,2,64,512]{4,3,2,1,0:T(8,128)(2,1)} %get-tuple-element.135), channel_id=1, source_target_pairs={{1,0},{2,1},{3,2},{4,3},{5,4},{6,5},{7,6},{9,8},{10,9},{11,10},{12... | collective-permute-start | bytes 1572872 | tf_op jit(solution)/shard_map/ppermute | solution.py:339
  82.3 11.7 %collective-permute-start.10 = (bf16[2,64,512]{2,1,0:T(8,128)(2,1)S(1)}, bf16[2,64,512]{2,1,0:T(8,128)(2,1)S(1)}, u32[]{:S(2)}, u32[]{:S(2)}) collective-permute-start(bf16[2,64,512]{2,1,0:T(8,128)(2,1)S(1)} %get-tuple-element.153), channel_id=1, source_target_pairs={{1,0},{2,1},{3,2},{4,3},{5,4},{6,5},{7,6},{9,8},{10,9},{11,10},{12... | collective-permute-start | bytes 393224 | tf_op jit(solution)/shard_map/ppermute | solution.py:339
  83.6 10.7 %collective-permute-start.9 = (bf16[2,64,512]{2,1,0:T(8,128)(2,1)S(1)}, bf16[2,64,512]{2,1,0:T(8,128)(2,1)S(1)}, u32[]{:S(2)}, u32[]{:S(2)}) collective-permute-start(bf16[2,64,512]{2,1,0:T(8,128)(2,1)S(1)} %get-tuple-element.154), channel_id=1, source_target_pairs={{0,1},{1,2},{2,3},{3,4},{4,5},{5,6},{6,7},{8,9},{9,10},{10,11},{11... | collective-permute-start | bytes 393224 | tf_op jit(solution)/shard_map/ppermute | solution.py:338
  96.1 64.5 %collective-permute-start.14 = (bf16[32,64,512]{2,1,0:T(8,128)(2,1)}, bf16[32,64,512]{2,1,0:T(8,128)(2,1)}, u32[]{:S(2)}, u32[]{:S(2)}) collective-permute-start(bf16[32,64,512]{2,1,0:T(8,128)(2,1)} %get-tuple-element.85), channel_id=1, source_target_pairs={{16,8},{24,16},{17,9},{25,17},{18,10},{26,18},{19,11},{27,19},{20,... | collective-permute-start | bytes 6291464 | tf_op jit(solution)/shard_map/ppermute | solution.py:344
  98.1 6.3 %collective-permute-start.6 = (bf16[2,64,512]{2,1,0:T(8,128)(2,1)S(1)}, bf16[2,64,512]{2,1,0:T(8,128)(2,1)S(1)}, u32[]{:S(2)}, u32[]{:S(2)}) collective-permute-start(bf16[2,64,512]{2,1,0:T(8,128)(2,1)S(1)} %get-tuple-element.156), channel_id=1, source_target_pairs={{0,1},{1,2},{2,3},{3,4},{4,5},{5,6},{6,7},{8,9},{9,10},{10,11},{11... | collective-permute-start | bytes 393224 | tf_op jit(solution)/shard_map/ppermute | solution.py:338
  102.4 9.5 %collective-permute-start.7 = (bf16[2,64,512]{2,1,0:T(8,128)(2,1)S(1)}, bf16[2,64,512]{2,1,0:T(8,128)(2,1)S(1)}, u32[]{:S(2)}, u32[]{:S(2)}) collective-permute-start(bf16[2,64,512]{2,1,0:T(8,128)(2,1)S(1)} %get-tuple-element.155), channel_id=1, source_target_pairs={{1,0},{2,1},{3,2},{4,3},{5,4},{6,5},{7,6},{9,8},{10,9},{11,10},{12... | collective-permute-start | bytes 393224 | tf_op jit(solution)/shard_map/ppermute | solution.py:339
  132.5 47.3 %collective-permute-start.11 = (bf16[32,64,512]{2,1,0:T(8,128)(2,1)}, bf16[32,64,512]{2,1,0:T(8,128)(2,1)S(1)}, u32[]{:S(2)}, u32[]{:S(2)}) collective-permute-start(bf16[32,64,512]{2,1,0:T(8,128)(2,1)} %get-tuple-element.80), channel_id=1, source_target_pairs={{0,8},{8,16},{1,9},{9,17},{2,10},{10,18},{3,11},{11,19},{4,12},{12... | collective-permute-start | bytes 6291464 | tf_op jit(solution)/shard_map/ppermute | solution.py:344
  161.6 18.3 %collective-permute-start.15 = (bf16[2,64,512]{2,1,0:T(8,128)(2,1)S(1)}, bf16[2,64,512]{2,1,0:T(8,128)(2,1)S(1)}, u32[]{:S(2)}, u32[]{:S(2)}) collective-permute-start(bf16[2,64,512]{2,1,0:T(8,128)(2,1)S(1)} %get-tuple-element.150), channel_id=1, source_target_pairs={{0,1},{1,2},{2,3},{3,4},{4,5},{5,6},{6,7},{8,9},{9,10},{10,11},{11... | collective-permute-start | bytes 393224 | tf_op jit(solution)/shard_map/ppermute | solution.py:338
  166.7 13.1 %collective-permute-start.16 = (bf16[2,64,512]{2,1,0:T(8,128)(2,1)S(1)}, bf16[2,64,512]{2,1,0:T(8,128)(2,1)S(1)}, u32[]{:S(2)}, u32[]{:S(2)}) collective-permute-start(bf16[2,64,512]{2,1,0:T(8,128)(2,1)S(1)} %get-tuple-element.149), channel_id=1, source_target_pairs={{1,0},{2,1},{3,2},{4,3},{5,4},{6,5},{7,6},{9,8},{10,9},{11,10},{12... | collective-permute-start | bytes 393224 | tf_op jit(solution)/shard_map/ppermute | solution.py:339
  181.3 72.5 %collective-permute-start.20 = (bf16[32,64,512]{2,1,0:T(8,128)(2,1)}, bf16[32,64,512]{2,1,0:T(8,128)(2,1)}, u32[]{:S(2)}, u32[]{:S(2)}) collective-permute-start(bf16[32,64,512]{2,1,0:T(8,128)(2,1)} %get-tuple-element.98), channel_id=1, source_target_pairs={{8,0},{16,8},{9,1},{17,9},{10,2},{18,10},{11,3},{19,11},{12,4},{20... | collective-permute-start | bytes 6291464 | tf_op jit(solution)/shard_map/ppermute | solution.py:344
  182.6 6.7 %collective-permute-start.12 = (bf16[2,64,512]{2,1,0:T(8,128)(2,1)S(1)}, bf16[2,64,512]{2,1,0:T(8,128)(2,1)S(1)}, u32[]{:S(2)}, u32[]{:S(2)}) collective-permute-start(bf16[2,64,512]{2,1,0:T(8,128)(2,1)S(1)} %get-tuple-element.152), channel_id=1, source_target_pairs={{0,1},{1,2},{2,3},{3,4},{4,5},{5,6},{6,7},{8,9},{9,10},{10,11},{11... | collective-permute-start | bytes 393224 | tf_op jit(solution)/shard_map/ppermute | solution.py:338
  187.3 5.2 %collective-permute-start.13 = (bf16[2,64,512]{2,1,0:T(8,128)(2,1)S(1)}, bf16[2,64,512]{2,1,0:T(8,128)(2,1)S(1)}, u32[]{:S(2)}, u32[]{:S(2)}) collective-permute-start(bf16[2,64,512]{2,1,0:T(8,128)(2,1)S(1)} %get-tuple-element.151), channel_id=1, source_target_pairs={{1,0},{2,1},{3,2},{4,3},{5,4},{6,5},{7,6},{9,8},{10,9},{11,10},{12... | collective-permute-start | bytes 393224 | tf_op jit(solution)/shard_map/ppermute | solution.py:339
  194.0 69.8 %collective-permute-start.17 = (bf16[32,64,512]{2,1,0:T(8,128)(2,1)}, bf16[32,64,512]{2,1,0:T(8,128)(2,1)S(1)}, u32[]{:S(2)}, u32[]{:S(2)}) collective-permute-start(bf16[32,64,512]{2,1,0:T(8,128)(2,1)} %get-tuple-element.93), channel_id=1, source_target_pairs={{8,16},{16,24},{9,17},{17,25},{10,18},{18,26},{11,19},{19,27},{12,... | collective-permute-start | bytes 6291464 | tf_op jit(solution)/shard_map/ppermute | solution.py:344
  254.7 9.0 %collective-permute-start.21 = (bf16[2,64,512]{2,1,0:T(8,128)(2,1)S(1)}, bf16[2,64,512]{2,1,0:T(8,128)(2,1)S(1)}, u32[]{:S(2)}, u32[]{:S(2)}) collective-permute-start(bf16[2,64,512]{2,1,0:T(8,128)(2,1)S(1)} %get-tuple-element.146), channel_id=1, source_target_pairs={{0,1},{1,2},{2,3},{3,4},{4,5},{5,6},{6,7},{8,9},{9,10},{10,11},{11... | collective-permute-start | bytes 393224 | tf_op jit(solution)/shard_map/ppermute | solution.py:338
  261.8 4.8 %collective-permute-start.22 = (bf16[2,64,512]{2,1,0:T(8,128)(2,1)S(1)}, bf16[2,64,512]{2,1,0:T(8,128)(2,1)S(1)}, u32[]{:S(2)}, u32[]{:S(2)}) collective-permute-start(bf16[2,64,512]{2,1,0:T(8,128)(2,1)S(1)} %get-tuple-element.145), channel_id=1, source_target_pairs={{1,0},{2,1},{3,2},{4,3},{5,4},{6,5},{7,6},{9,8},{10,9},{11,10},{12... | collective-permute-start | bytes 393224 | tf_op jit(solution)/shard_map/ppermute | solution.py:339
  287.2 77.6 %collective-permute-start.26 = (bf16[32,64,512]{2,1,0:T(8,128)(2,1)}, bf16[32,64,512]{2,1,0:T(8,128)(2,1)S(1)}, u32[]{:S(2)}, u32[]{:S(2)}) collective-permute-start(bf16[32,64,512]{2,1,0:T(8,128)(2,1)} %get-tuple-element.111), channel_id=1, source_target_pairs={{8,0},{9,1},{10,2},{11,3},{12,4},{13,5},{14,6},{15,7}} | collective-permute-start | bytes 6291464 | tf_op jit(solution)/shard_map/ppermute | solution.py:344
  289.5 7.4 %collective-permute-start.18 = (bf16[2,64,512]{2,1,0:T(8,128)(2,1)S(1)}, bf16[2,64,512]{2,1,0:T(8,128)(2,1)S(1)}, u32[]{:S(2)}, u32[]{:S(2)}) collective-permute-start(bf16[2,64,512]{2,1,0:T(8,128)(2,1)S(1)} %get-tuple-element.148), channel_id=1, source_target_pairs={{0,1},{1,2},{2,3},{3,4},{4,5},{5,6},{6,7},{8,9},{9,10},{10,11},{11... | collective-permute-start | bytes 393224 | tf_op jit(solution)/shard_map/ppermute | solution.py:338
  299.6 70.4 %collective-permute-start.23 = (bf16[32,64,512]{2,1,0:T(8,128)(2,1)}, bf16[32,64,512]{2,1,0:T(8,128)(2,1)}, u32[]{:S(2)}, u32[]{:S(2)}) collective-permute-start(bf16[32,64,512]{2,1,0:T(8,128)(2,1)} %get-tuple-element.106), channel_id=1, source_target_pairs={{16,24},{17,25},{18,26},{19,27},{20,28},{21,29},{22,30},{23,31}} | collective-permute-start | bytes 6291464 | tf_op jit(solution)/shard_map/ppermute | solution.py:344
  364.8 17.8 %collective-permute-start.27 = (bf16[2,64,512]{2,1,0:T(8,128)(2,1)S(1)}, bf16[2,64,512]{2,1,0:T(8,128)(2,1)S(1)}, u32[]{:S(2)}, u32[]{:S(2)}) collective-permute-start(bf16[2,64,512]{2,1,0:T(8,128)(2,1)S(1)} %get-tuple-element.142), channel_id=1, source_target_pairs={{0,1},{1,2},{2,3},{3,4},{4,5},{5,6},{6,7},{8,9},{9,10},{10,11},{11... | collective-permute-start | bytes 393224 | tf_op jit(solution)/shard_map/ppermute | solution.py:338
  368.7 14.0 %collective-permute-start.28 = (bf16[2,64,512]{2,1,0:T(8,128)(2,1)S(1)}, bf16[2,64,512]{2,1,0:T(8,128)(2,1)S(1)}, u32[]{:S(2)}, u32[]{:S(2)}) collective-permute-start(bf16[2,64,512]{2,1,0:T(8,128)(2,1)S(1)} %get-tuple-element.141), channel_id=1, source_target_pairs={{1,0},{2,1},{3,2},{4,3},{5,4},{6,5},{7,6},{9,8},{10,9},{11,10},{12... | collective-permute-start | bytes 393224 | tf_op jit(solution)/shard_map/ppermute | solution.py:339
  371.0 32.3 %collective-permute-start.24 = (bf16[2,64,512]{2,1,0:T(8,128)(2,1)S(1)}, bf16[2,64,512]{2,1,0:T(8,128)(2,1)S(1)}, u32[]{:S(2)}, u32[]{:S(2)}) collective-permute-start(bf16[2,64,512]{2,1,0:T(8,128)(2,1)S(1)} %get-tuple-element.144), channel_id=1, source_target_pairs={{0,1},{1,2},{2,3},{3,4},{4,5},{5,6},{6,7},{8,9},{9,10},{10,11},{11... | collective-permute-start | bytes 393224 | tf_op jit(solution)/shard_map/ppermute | solution.py:338
  380.8 22.6 %collective-permute-start.25 = (bf16[2,64,512]{2,1,0:T(8,128)(2,1)S(1)}, bf16[2,64,512]{2,1,0:T(8,128)(2,1)S(1)}, u32[]{:S(2)}, u32[]{:S(2)}) collective-permute-start(bf16[2,64,512]{2,1,0:T(8,128)(2,1)S(1)} %get-tuple-element.143), channel_id=1, source_target_pairs={{1,0},{2,1},{3,2},{4,3},{5,4},{6,5},{7,6},{9,8},{10,9},{11,10},{12... | collective-permute-start | bytes 393224 | tf_op jit(solution)/shard_map/ppermute | solution.py:339
  422.8 4.1 collective-permute-start.29
  428.3 10.4 %collective-permute-start.30 = (bf16[153,1024]{1,0:T(8,128)(2,1)S(1)}, bf16[153,1024]{1,0:T(8,128)(2,1)S(1)}, u32[]{:S(2)}, u32[]{:S(2)}) collective-permute-start(bf16[153,1024]{1,0:T(8,128)(2,1)S(1)} %pad_maximum_fusion.5), channel_id=1, source_target_pairs={{0,2},{1,3},{2,0},{3,1},{4,6},{5,7},{6,4},{7,5},{8,10},{9,11},{10,... | collective-permute-start | bytes 940040 | tf_op jit(solution)/shard_map/ppermute | solution.py:360
  439.9 11.8 %collective-permute-start.31 = (bf16[89,1024]{1,0:T(8,128)(2,1)S(1)}, bf16[89,1024]{1,0:T(8,128)(2,1)S(1)}, u32[]{:S(2)}, u32[]{:S(2)}) collective-permute-start(bf16[89,1024]{1,0:T(8,128)(2,1)S(1)} %pad_maximum_fusion.6), channel_id=1, source_target_pairs={{0,4},{1,5},{2,6},{3,7},{4,0},{5,1},{6,2},{7,3},{8,12},{9,13},{10,... | collective-permute-start | bytes 546824 | tf_op jit(solution)/shard_map/ppermute | solution.py:360
  452.7 15.8 %collective-permute-start.32 = (bf16[89,512]{1,0:T(8,128)(2,1)S(1)}, bf16[89,512]{1,0:T(8,128)(2,1)S(1)}, u32[]{:S(2)}, u32[]{:S(2)}) collective-permute-start(bf16[89,512]{1,0:T(8,128)(2,1)S(1)} %pad_maximum_fusion.8), channel_id=1, source_target_pairs={{0,24},{8,16},{16,8},{24,0},{1,25},{9,17},{17,9},{25,1},{2,26},{10... | collective-permute-start | bytes 273416 | tf_op jit(solution)/shard_map/ppermute | solution.py:457
  (32 other events, 190.9 us)
